TPU v7x, 32 devices: a whole 2x2x4 slice. The times are simulated.
32 devices in a mesh: groups: 2 (over y), ctx: 8 (over z, core), heads: 2 (over x).
Axes of the slice: x: 2, y: 2, z: 4, core: 2. Of those that a mesh axis runs over, the one named last changes fastest.
Arguments:
- queries: bfloat16 [4096, 8192], P(('groups', 'ctx'), 'heads'), parts along dimension 0, may hold values from -32 to 32, as said below
- keys: bfloat16 [4096, 1024], P(('groups', 'ctx'), 'heads'), parts along dimension 0, may hold values from -32 to 32, as said below
- values: bfloat16 [4096, 1024], P(('groups', 'ctx'), 'heads'), parts along dimension 0, may hold values from -6 to 6
- doc_ids: int32 [4096], P('groups'), parts along dimension 0, may hold values from 0 to 17, never falling along the last dimension, each value on 1 to 1024 neighbouring positions
- block_mask: int32 [32, 16], P('groups'), parts along dimension 0, may hold values from 0 to 1, as said below
- out_weight: bfloat16 [8192, 8192], P('heads', 'ctx'), may hold values from -0.5 to 0.5
Outputs:
- mixed: bfloat16 [4096, 8192], P(('groups', 'ctx'), 'heads'), parts along dimension 0
There are 2 independent parts, one for each index of `groups`. A program takes and returns all parts, laid end to end along the dimension named above; an argument that names none is the same for every part. Nothing has to cross between parts.
Inputs may be any that keep to these rules, and one draw needn't show every extreme that they name: `queries`: entries lie within the stated bounds. `keys`: entries lie within the stated bounds. `block_mask`: zero on and above the diagonal; the last block may read the first.
All inputs are finite; a program needn't handle non-finite values.
Results may differ from a plain program's by a relative error of at most 0.009.
Values may be sent and summed in bfloat16 or wider, within the bound.
No kernel may reach another device: no remote copies, remote signals or barrier semaphores. Data moves between devices by JAX's collectives and lax.ppermute only.
A program may use at most 256 MiB of HBM per device.

v0:
```python
import functools
import jax, jax.numpy as jnp
from jax import lax
from jax.experimental import pallas as pl
from jax.experimental.pallas import tpu as pltpu
from jax.sharding import PartitionSpec as P


HEADS = 64
KVH = 8
GROUP = HEADS // KVH
TOGETHER = 4
HD = 128
BLOCK = 128
NEG = -1e30
LANES = ("ctx", "heads")


def attn_body(cores, skip, meta, dlast, links, docq, dock, q, *rest):
    nkv = len(rest) - 7
    kvs = rest[:nkv]
    out, kv, acc, peak, stack, todo, sem = rest[nkv:]
    j, b = pl.program_id(0), pl.program_id(1)
    per_dev = kv.shape[1]
    place = meta[0]
    core = lax.rem(place, cores)
    chip = lax.div(place, cores)
    nb = dlast.shape[0]
    hops = nkv // cores
    mine = place * per_dev + b

    @pl.when((j == 0) & (b == 0))
    def _():
        for i in range(nkv):
            for r in range(per_dev):
                pltpu.make_async_copy(kvs[i].at[pl.ds(r * BLOCK, BLOCK)], kv.at[i, r], sem.at[i, r]).start()
        for i in range(nkv):
            for r in range(per_dev):
                pltpu.make_async_copy(kvs[i].at[pl.ds(r * BLOCK, BLOCK)], kv.at[i, r], sem.at[i, r]).wait()

    @pl.when(j == 0)
    def _():
        todo[b, 0] = mine

        def scan(t, n):
            on = (links[b * nb + t] > 0) | (dlast[t] == meta[1 + b])
            todo[b, n] = t
            return n + on.astype(jnp.int32)

        n = lax.fori_loop(0, mine, scan, jnp.int32(1))
        todo[b, n] = mine
        todo[b, nb + 1] = n

    count = todo[b, nb + 1]

    acc[...] = jnp.zeros_like(acc)
    peak[...] = jnp.full_like(peak, NEG)
    for g in range(GROUP):
        stack[g * BLOCK : (g + 1) * BLOCK] = q[:, g * HD : (g + 1) * HD]
    dq = docq[...]
    rows = lax.broadcasted_iota(jnp.int32, (BLOCK, BLOCK), 0)
    cols = lax.broadcasted_iota(jnp.int32, (BLOCK, BLOCK), 1)
    c = HD ** -0.5 * 1.4426950408889634
    kcol = pl.ds(pl.multiple_of((skip + j) * HD, HD), HD)
    vcol = pl.ds(pl.multiple_of((kv.shape[3] // (2 * HD) + skip + j) * HD, HD), HD)

    def fetch(i):
        t = todo[b, i]
        dev = lax.div(t, per_dev)
        slot = (chip - lax.div(dev, cores)) + hops * (lax.rem(dev, cores) != core).astype(jnp.int32)
        r = lax.rem(t, per_dev)
        dk = dock[pl.ds(t, 1), :]
        ok = (dq == dk) | (links[b * nb + t] > 0)
        ok = ok & (rows + (mine - t) * BLOCK >= cols) & (i < count)
        return kv[slot, r, :, kcol], kv[slot, r, :, vcol], jnp.where(ok, 0.0, NEG)

    ones = jnp.ones((2 * BLOCK, HD), jnp.bfloat16)
    rows_of = TOGETHER * BLOCK

    def step(i, carry):
        k0, v0, b0 = fetch(2 * i)
        k1, v1, b1 = fetch(2 * i + 1)
        keys = jnp.concatenate([k0, k1], 0)
        vals = jnp.concatenate([jnp.concatenate([v0, v1], 0), ones], 1)
        bias = jnp.concatenate([b0, b1], 1)
        bias = jnp.concatenate([bias] * TOGETHER, 0)
        for g in range(GROUP // TOGETHER):
            at = slice(g * rows_of, (g + 1) * rows_of)
            s = lax.dot_general(stack[at], keys, (((1,), (1,)), ((), ())), preferred_element_type=jnp.float32)
            s = s + bias
            old = peak[at]
            top = jnp.maximum(old, jnp.max(s, axis=1, keepdims=True))
            fac = jnp.exp2((old - top) * c)
            p = jnp.exp2((s - jnp.concatenate([top, top], 1)) * c).astype(jnp.bfloat16)
            w = jnp.dot(p, vals, preferred_element_type=jnp.float32)
            acc[at] = acc[at] * jnp.concatenate([fac, fac], 1) + w
            peak[at] = top
        return carry

    lax.fori_loop(0, lax.div(count + 1, 2), step, 0)
    for g in range(GROUP):
        a = acc[g * BLOCK : (g + 1) * BLOCK]
        out[:, g * HD:(g + 1) * HD] = (a[:, :HD] / a[:, HD:]).astype(out.dtype)


def attention(q, kvs, place, docs, mask, cores, skip=0):
    tok, width = q.shape
    kvh = width // (GROUP * HD)
    per_dev = tok // BLOCK
    nb = mask.shape[0]
    dock = docs.reshape(nb, BLOCK)
    dlast = dock[:, -1]
    own = lax.dynamic_slice_in_dim(dock, place * per_dev, per_dev)
    meta = jnp.concatenate([place[None].astype(jnp.int32), own[:, 0]])
    links = lax.dynamic_slice_in_dim(mask, place * per_dev, per_dev).reshape(-1)
    docq = jnp.broadcast_to(own.reshape(tok, 1), (tok, BLOCK))
    n = len(kvs)
    grid_spec = pltpu.PrefetchScalarGridSpec(
        num_scalar_prefetch=3, grid=(kvh, per_dev),
        in_specs=[
            pl.BlockSpec((BLOCK, BLOCK), lambda j, b, *_: (b, 0)),
            pl.BlockSpec((nb, BLOCK), lambda j, b, *_: (0, 0)),
            pl.BlockSpec((BLOCK, GROUP * HD), lambda j, b, *_: (b, j)),
        ] + [pl.BlockSpec(memory_space=pl.ANY)] * n,
        out_specs=pl.BlockSpec((BLOCK, GROUP * HD), lambda j, b, *_: (b, j)),
        scratch_shapes=[
            pltpu.VMEM((n, per_dev, BLOCK, kvs[0].shape[1]), jnp.bfloat16),
            pltpu.VMEM((GROUP * BLOCK, 2 * HD), jnp.float32),
            pltpu.VMEM((GROUP * BLOCK, HD), jnp.float32),
            pltpu.VMEM((GROUP * BLOCK, HD), jnp.bfloat16),
            pltpu.SMEM((per_dev, nb + 2), jnp.int32),
            pltpu.SemaphoreType.DMA((n, per_dev)),
        ])
    return pl.pallas_call(
        functools.partial(attn_body, cores, skip), grid_spec=grid_spec,
        out_shape=jax.ShapeDtypeStruct((tok, width), jnp.bfloat16),
        name="attend",
        cost_estimate=pl.CostEstimate(flops=2*tok*width*nb*BLOCK, bytes_accessed=4 << 20, transcendentals=tok*width//HD*nb*BLOCK//2),
    )(meta, dlast, links, docq, dock, q, *kvs)


SENT = (2, 2)
UNITS = ((0, 0, 2), (1, 0, 2))


def project_body(mode, tiles, count, both, twin, meta, *rest):
    ins = rest[: 2 * count if both else count]
    rest = rest[len(ins) :]
    if mode == "rest":
        part, rest = rest[0], rest[1:]
    weights, rest = rest[: len(tiles)], rest[len(tiles) :]
    outs, (left, sem) = rest[:-2], rest[-2:]
    i = pl.program_id(0)
    half = left.shape[1] // count

    @pl.when(i == 0)
    def _():
        def load(group):
            tok = group[0].shape[0]
            copies = [
                pltpu.make_async_copy(
                    x,
                    left.at[pl.ds(n // count * tok, tok), pl.ds(n % count * half, half)],
                    sem.at[n],
                )
                for n, x in enumerate(group)
            ]
            for copy in copies:
                copy.start()
            for copy in copies:
                copy.wait()

        if not both:
            load(ins)
        else:
            one, two = ins[:count], ins[count:]
            pl.when(meta[0] == 0)(lambda: load(one + two if twin else one))
            pl.when(meta[0] != 0)(lambda: load(two + one if twin else two))

    def store(w):
        res = jnp.dot(left[...], w[...], preferred_element_type=jnp.float32)
        if mode == "rest":
            res = res + part[...]
        if mode in ("full", "part"):
            outs[0][...] = res.astype(outs[0].dtype)
            return
        res = res.astype(jnp.bfloat16)
        rows = res.shape[0] // (4 if twin else 2)
        first = meta[1] == 0
        for n in range(2 if twin else 1):
            at = slice(n * rows, (n + 1) * rows)
            top, low = res[2 * n * rows : (2 * n + 1) * rows], res[(2 * n + 1) * rows : (2 * n + 2) * rows]
            outs[0][at] = jnp.where(first, top, low)
            outs[1][at] = jnp.where(first, low, top)

    begin = 0
    for w, n in zip(weights, tiles):
        pl.when((i >= begin) & (i < begin + n))(lambda w=w: store(w))
        begin += n


def project(mode, pick, side, a, b, weights, row=None, part=None, twin=False):
    tok = a[0].shape[0] * (2 if twin else 1)
    cols = weights[0].shape[1]
    depth = sum(x.shape[1] for x in a)
    at = 0 if row is None else row
    step = 512
    per = cols // step
    tiles = [per] * len(weights)
    total = cols * len(weights)
    meta = jnp.stack([pick.astype(jnp.int32), side.astype(jnp.int32)])
    anywhere = pl.BlockSpec(memory_space=pl.ANY)
    ins = list(a) + list(b)
    specs = [anywhere] * len(ins)
    if part is not None:
        array, first = part
        ins.append(array)
        specs.append(pl.BlockSpec((tok, step), lambda i, *_: (0, first + i)))
    for n, w in enumerate(weights):
        ins.append(w)
        specs.append(
            pl.BlockSpec((depth, step), lambda i, *_, n=n: (at, jnp.clip(i - n * per, 0, per - 1)))
        )
    if mode in ("full", "part"):
        kind = jnp.bfloat16 if mode == "full" else jnp.float32
        outs = jax.ShapeDtypeStruct((tok, total), kind)
        out_specs = pl.BlockSpec((tok, step), lambda i, *_: (0, i))
    else:
        outs = [jax.ShapeDtypeStruct((tok // 2, total), jnp.bfloat16)] * 2
        out_specs = [pl.BlockSpec((tok // 2, step), lambda i, *_: (0, i))] * 2
    grid_spec = pltpu.PrefetchScalarGridSpec(
        num_scalar_prefetch=1,
        grid=(per * len(weights),),
        in_specs=specs,
        out_specs=out_specs,
        scratch_shapes=[
            pltpu.VMEM((tok, depth), jnp.bfloat16),
            pltpu.SemaphoreType.DMA((2 * len(a),)),
        ],
    )
    return pl.pallas_call(
        functools.partial(project_body, mode, tiles, len(a), bool(b), twin),
        grid_spec=grid_spec,
        out_shape=outs,
        cost_estimate=pl.CostEstimate(
            flops=2 * tok * depth * total, bytes_accessed=2 * depth * total, transcendentals=0
        ),
        compiler_params=pltpu.CompilerParams(vmem_limit_bytes=40 << 20),
    )(meta, *ins)


NAMES = ("first", "again", "second", "third", "own")
HOPS = {
    "first": [(0, 1), (1, 2), (2, 1), (3, 2)],
    "again": [(1, 0), (2, 3)],
    "second": [(0, 2), (1, 3), (2, 0), (3, 1)],
    "third": [(0, 3), (3, 0)],
    "own": [(z, z) for z in range(4)],
}


def spots_of(name, piece):
    return [(h, t) for h in range(2) for t in range(4) if (2 * h + piece, t) in HOPS[name]]


def any_of(spots, chip, side):
    return functools.reduce(jnp.logical_or, [(chip == t) & (side == h) for h, t in spots])


def block_at(out, core, side, piece, other, row):
    rows, cols = out.shape[0] // 2, out.shape[1] // 4
    block = piece * 2 + jnp.where(core == 0, other, 1 - other)
    at = pl.ds(pl.multiple_of(block * cols, cols), cols)
    if row is None:
        return out.at[:, at]
    half = side if row == 0 else 1 - side
    return out.at[pl.ds(pl.multiple_of(half * rows, rows), rows), at]


def collect_body(meta, *refs):
    ins, (out, sem) = refs[:-2], refs[-2:]
    got = {n: ins[2 * i : 2 * i + 2] for i, n in enumerate(NAMES[:3])}
    own = ins[6]
    chip, side, core = meta[0], meta[1], meta[2]
    cols = out.shape[1] // 4

    def copies(name, piece):
        made = []
        for o in range(2):
            at = pl.ds(o * cols, cols)
            if name == "own":
                dst = block_at(out, core, side, piece, o, None)
                made.append(pltpu.make_async_copy(own.at[:, at], dst, sem.at[piece, o]))
                continue
            for r in range(2):
                dst = block_at(out, core, side, piece, o, r)
                src = got[name][r].at[:, at]
                made.append(pltpu.make_async_copy(src, dst, sem.at[piece, 2 * o + r]))
        return made

    todo = [(p, n) for p in range(2) for n in ("first", "again", "second", "own")]
    todo = [(p, n, any_of(spots_of(n, p), chip, side)) for p, n in todo if spots_of(n, p)]
    for p, n, hit in todo:
        pl.when(hit)(lambda p=p, n=n: [c.start() for c in copies(n, p)] and None)
    for p, n, hit in todo:
        pl.when(hit)(lambda p=p, n=n: [c.wait() for c in copies(n, p)] and None)


def finish_body(meta, *refs):
    third, (_, out, held, sem) = refs[:4], refs[4:]
    chip, side, core = meta[0], meta[1], meta[2]
    for piece in range(2):
        spots = spots_of("third", piece)

        @pl.when(any_of(spots, chip, side))
        def _(piece=piece):
            into = [
                pltpu.make_async_copy(third[n], held.at[n], sem.at[n]) for n in range(4)
            ]
            back = [
                pltpu.make_async_copy(
                    held.at[n], block_at(out, core, side, piece, n // 2, n % 2), sem.at[n]
                )
                for n in range(4)
            ]
            for copy in into:
                copy.start()
            for one, two in zip(into, back):
                one.wait()
                two.start()
            for copy in back:
                copy.wait()


def collect(chip, side, core, arrays, tok, cols):
    meta = jnp.stack([chip, side, core]).astype(jnp.int32)
    return pl.pallas_call(
        collect_body,
        grid_spec=pltpu.PrefetchScalarGridSpec(
            num_scalar_prefetch=1,
            grid=(),
            in_specs=[pl.BlockSpec(memory_space=pl.ANY)] * len(arrays),
            out_specs=pl.BlockSpec((tok, cols), lambda *_: (0, 0)),
            scratch_shapes=[pltpu.SemaphoreType.DMA((2, 4))],
        ),
        out_shape=jax.ShapeDtypeStruct((tok, cols), jnp.bfloat16),
        name="collect",
    )(meta, *arrays)


def finish(chip, side, core, arrays, out):
    meta = jnp.stack([chip, side, core]).astype(jnp.int32)
    anywhere = pl.BlockSpec(memory_space=pl.ANY)
    return pl.pallas_call(
        finish_body,
        grid_spec=pltpu.PrefetchScalarGridSpec(
            num_scalar_prefetch=1,
            grid=(),
            in_specs=[anywhere] * (len(arrays) + 1),
            out_specs=anywhere,
            scratch_shapes=[
                pltpu.VMEM((4,) + arrays[0].shape, jnp.bfloat16),
                pltpu.SemaphoreType.DMA((4,)),
            ],
        ),
        out_shape=jax.ShapeDtypeStruct(out.shape, out.dtype),
        input_output_aliases={len(arrays) + 1: 0},
        name="finish",
    )(meta, *arrays, out)


def line(x, hop):
    n = lax.axis_size("ctx")
    pairs = [(i, i + 2 * hop) for i in range(n) if 0 <= i + 2 * hop < n]
    return lax.ppermute(x, "ctx", pairs)


def partner(x):
    return lax.ppermute(x, "ctx", [(i, i ^ 1) for i in range(lax.axis_size("ctx"))])


def across(x):
    return lax.ppermute(x, "heads", [(0, 1), (1, 0)])


def parts_of(keys, values, heads):
    out, at = [], 0
    for n in heads:
        cut = slice(at * HD, (at + n) * HD)
        out.append(jnp.concatenate([keys[:, cut], values[:, cut]], axis=1))
        at += n
    return out


def send_back(slot, total):
    straight, crossed = [], []
    for z, t in HOPS[slot]:
        for k in range(2):
            for h in range(2):
                pair = ((2 * z + k) * 2 + h, (2 * t + k) * 2 + z // 2)
                (straight if h == z // 2 else crossed).append(pair)
    one = lax.ppermute(total, LANES, straight)
    two = lax.ppermute(total, LANES, crossed)
    return one, two


def on_line(queries, keys, values, doc_ids, block_mask, out_weight):
    place = lax.axis_index("ctx")
    side = lax.axis_index("heads")
    chip = place // 2
    core = place % 2
    tok = queries.shape[0]
    kv = parts_of(keys, values, SENT)
    near = [[kv[f]] + [line(kv[f], s) for s in range(1, 4)] for f in range(len(kv))]
    w_other = partner(out_weight)
    whole = [near[f] + [partner(x) for x in near[f]] for f in range(len(kv))]
    attn, ups, downs = [], [[] for _ in range(3)], [[] for _ in range(3)]
    left = 0
    for f, skip, n in UNITS:
        wide = n * GROUP * HD
        out = attention(
            queries[:, left : left + wide], whole[f], place, doc_ids, block_mask, 2, skip
        )
        left += wide
        attn.append(out)
        up = down = out
        for s in range(3):
            up = line(up, 1)
            down = line(down, -1)
            ups[s].append(up)
            downs[s].append(down)

    low = chip < 2
    zero = jnp.int32(0)
    pair = [out_weight, w_other]

    own = project("full", zero, zero, attn, [], pair)
    goes = [
        ((2 * z + k) * 2 + (1 - z // 2), (2 * z + k) * 2 + z // 2)
        for z in range(4)
        for k in range(2)
    ]
    moved = lax.ppermute(own, LANES, goes)
    arrays = []
    keep, send = project("split", ~low, side, downs[0], ups[0], pair, twin=True)
    both = keep + across(send)
    arrays += send_back("first", both[: tok // 2])
    arrays += send_back("again", both[tok // 2 :])
    keep, send = project("split", ~low, side, downs[1], ups[1], pair)
    arrays += send_back("second", keep + across(send))
    own = own + moved
    out = collect(chip, side, core, arrays + [own], tok, queries.shape[1])
    early = project("part", ~low, side, downs[2][:-1], ups[2][:-1], pair, row=0)
    cols = out_weight.shape[1]
    thirds = []
    for o in range(2):
        keep, send = project(
            "rest",
            ~low,
            side,
            downs[2][-1:],
            ups[2][-1:],
            pair[o : o + 1],
            row=1,
            part=(early, o * cols // 512),
        )
        thirds += send_back("third", keep + across(send))
    return finish(chip, side, core, thirds, out)


def gathered(queries, keys, values, doc_ids, block_mask, out_weight):
    place = lax.axis_index("ctx")
    n = lax.axis_size("ctx")
    kv = lax.all_gather(parts_of(keys, values, [keys.shape[1] // HD])[0], "ctx", axis=0)
    flip = place + 1 - 2 * (place % 2)

    def of(start):
        return [
            lax.dynamic_index_in_dim(kv, (start - 2 * s + n) % n, 0, keepdims=False)
            for s in range(n // 2)
        ]

    attn = attention(queries, of(place) + of(flip), place, doc_ids, block_mask, 2)
    partial_out = jnp.dot(
        attn,
        lax.all_gather(out_weight, "ctx", axis=1, tiled=True),
        preferred_element_type=jnp.float32,
    )
    return lax.psum_scatter(
        partial_out.astype(jnp.bfloat16), "heads", scatter_dimension=1, tiled=True
    )


def solution(mesh):
    in_specs = (
        P(("groups", "ctx"), "heads"),
        P(("groups", "ctx"), "heads"),
        P(("groups", "ctx"), "heads"),
        P("groups"),
        P("groups", None),
        P("heads", "ctx"),
    )
    out_specs = P(("groups", "ctx"), "heads")
    short = mesh.shape["ctx"] == 8 and mesh.shape["heads"] == 2

    def body(*args):
        return (on_line if short else gathered)(*args)

    return jax.shard_map(
        body, mesh=mesh, in_specs=in_specs, out_specs=out_specs, check_vma=False
    )
```

profile of v0, /device:TPU:17, one launch (start us, length us, event | category | flops | bytes accessed | tf_op | source)
XLA Modules:
  0.0 304.6 jit_solution(2964974799807881890)
XLA Ops:
  1.8 3.2 %collective-permute-start.13 = (bf16[256,512]{1,0:T(8,128)(2,1)S(1)}, bf16[256,512]{1,0:T(8,128)(2,1)S(1)}, u32[]{:S(2)}, u32[]{:S(2)}) collective-permute-start(bf16[256,512]{1,0:T(8,128)(2,1)S(1)} %pad_maximum_fusion.1.rest_0_), channel_id=1, source_target_pairs={{0,4},{2,6},{4,8},{6,10},{8,12},{10,14},{1,5},{3,7},{5,9},{7,11},{... | collective-permute-start | bytes 786440 | tf_op jit(solution)/shard_map/ppermute | solution.py:375
  7.6 3.9 %collective-permute-done.13.rest_1_ = bf16[256,512]{1,0:T(8,128)(2,1)S(1)} collective-permute-done((bf16[256,512]{1,0:T(8,128)(2,1)S(1)}, bf16[256,512]{1,0:T(8,128)(2,1)S(1)}, u32[]{:S(2)}, u32[]{:S(2)}) %collective-permute-start.13) | collective-permute-done | bytes 262176 | tf_op jit(solution)/shard_map/ppermute | solution.py:375
  11.6 3.1 %collective-permute-start = (bf16[256,512]{1,0:T(8,128)(2,1)S(1)}, bf16[256,512]{1,0:T(8,128)(2,1)S(1)}, u32[]{:S(2)}, u32[]{:S(2)}) collective-permute-start(bf16[256,512]{1,0:T(8,128)(2,1)S(1)} %pad_maximum_fusion.rest_0_), channel_id=1, source_target_pairs={{0,4},{2,6},{4,8},{6,10},{8,12},{10,14},{1,5},{3,7},{5,9},{7,11},{... | collective-permute-start | bytes 786440 | tf_op jit(solution)/shard_map/ppermute | solution.py:375
  14.6 2.3 collective-permute-done.14.rest_2_
  18.3 1.5 fusion
  20.5 9.4 %collective-permute-start.17 = (bf16[256,512]{1,0:T(8,128)(2,1)S(1)}, bf16[256,512]{1,0:T(8,128)(2,1)S(1)}, u32[]{:S(2)}, u32[]{:S(2)}) collective-permute-start(bf16[256,512]{1,0:T(8,128)(2,1)S(1)} %collective-permute-done.13.rest_1_), channel_id=1, source_target_pairs={{0,2},{2,0},{4,6},{6,4},{8,10},{10,8},{12,14},{14,12},{1,3},{3,1},... | collective-permute-start | bytes 786440 | tf_op jit(solution)/shard_map/ppermute | solution.py:379
  29.9 9.7 %collective-permute-done.rest_1_ = bf16[256,512]{1,0:T(8,128)(2,1)S(1)} collective-permute-done((bf16[256,512]{1,0:T(8,128)(2,1)S(1)}, bf16[256,512]{1,0:T(8,128)(2,1)S(1)}, u32[]{:S(2)}, u32[]{:S(2)}) %collective-permute-start) | collective-permute-done | bytes 262176 | tf_op jit(solution)/shard_map/ppermute | solution.py:375
  39.6 4.4 %collective-permute-start.18 = (bf16[256,512]{1,0:T(8,128)(2,1)S(1)}, bf16[256,512]{1,0:T(8,128)(2,1)}, u32[]{:S(2)}, u32[]{:S(2)}) collective-permute-start(bf16[256,512]{1,0:T(8,128)(2,1)S(1)} %collective-permute-done.14.rest_2_), channel_id=1, source_target_pairs={{0,2},{2,0},{4,6},{6,4},{8,10},{10,8},{12,14},{14,12},{1,3},{3,1},... | collective-permute-start | bytes 786440 | tf_op jit(solution)/shard_map/ppermute | solution.py:379
  48.0 12.0 %attend.3.rest_0_ = bf16[256,2048]{1,0:T(8,128)(2,1)} custom-call(s32[3]{0:T(128)} %pad_add_fusion.2.meta, s32[16]{0:T(128)} %slice_reduce_fusion.dlast, s32[32]{0:T(128)} %reshape.12.links, s32[256,128]{1,0:T(8,128)} %broadcast_in_dim.16.docq, s32[16,128]{1,0:T(8,128)} %bitcast.8, bf16[256,2048]{1,0:T(8,128)(2,1)} %get-tuple-element.21.q, ...), custom_call_target="tpu_custom_call" | custom-call | flops 2147483648 | bytes 4194304 | tf_op jit(solution)/shard_map/attend/pallas_call | solution.py:134
  60.0 12.8 %collective-permute-start.20 = (bf16[256,2048]{1,0:T(8,128)(2,1)}, bf16[256,2048]{1,0:T(8,128)(2,1)S(1)}, u32[]{:S(2)}, u32[]{:S(2)}) collective-permute-start(bf16[256,2048]{1,0:T(8,128)(2,1)} %attend.3.rest_0_), channel_id=1, source_target_pairs={{4,0},{6,2},{8,4},{10,6},{12,8},{14,10},{5,1},{7,3},{9,5},{11,7},{... | collective-permute-start | bytes 3145736 | tf_op jit(solution)/shard_map/ppermute | solution.py:375
  72.9 1.9 collective-permute-start.23
  74.8 12.0 %attend.2.rest_1_ = bf16[256,2048]{1,0:T(8,128)(2,1)} custom-call(s32[3]{0:T(128)} %pad_add_fusion.2.meta, s32[16]{0:T(128)} %slice_reduce_fusion.dlast, s32[32]{0:T(128)} %reshape.12.links, s32[256,128]{1,0:T(8,128)} %broadcast_in_dim.16.docq, s32[16,128]{1,0:T(8,128)} %bitcast.9, bf16[256,2048]{1,0:T(8,128)(2,1)} %get-tuple-element.22.q, ...), custom_call_target="tpu_custom_call" | custom-call | flops 2147483648 | bytes 4194304 | tf_op jit(solution)/shard_map/attend/pallas_call | solution.py:134
  86.8 1.9 collective-permute-start.10
  88.8 7.3 %collective-permute-start.7 = (bf16[256,2048]{1,0:T(8,128)(2,1)}, bf16[256,2048]{1,0:T(8,128)(2,1)}, u32[]{:S(2)}, u32[]{:S(2)}) collective-permute-start(bf16[256,2048]{1,0:T(8,128)(2,1)} %attend.2.rest_1_), channel_id=1, source_target_pairs={{4,0},{6,2},{8,4},{10,6},{12,8},{14,10},{5,1},{7,3},{9,5},{11,7},{... | collective-permute-start | bytes 3145736 | tf_op jit(solution)/shard_map/ppermute | solution.py:375
  96.0 4.4 %collective-permute-start.21 = (bf16[256,2048]{1,0:T(8,128)(2,1)S(1)}, bf16[256,2048]{1,0:T(8,128)(2,1)S(1)}, u32[]{:S(2)}, u32[]{:S(2)}) collective-permute-start(bf16[256,2048]{1,0:T(8,128)(2,1)S(1)} %collective-permute-done.20.rest_0_), channel_id=1, source_target_pairs={{4,0},{6,2},{8,4},{10,6},{12,8},{14,10},{5,1},{7,3},{9,5},{11,7},{... | collective-permute-start | bytes 3145736 | tf_op jit(solution)/shard_map/ppermute | solution.py:375
  100.4 1.9 collective-permute-start.24
  102.3 20.4 %collective-permute-done.10.rest_3_ = bf16[256,2048]{1,0:T(8,128)(2,1)} collective-permute-done((bf16[256,2048]{1,0:T(8,128)(2,1)}, bf16[256,2048]{1,0:T(8,128)(2,1)}, u32[]{:S(2)}, u32[]{:S(2)}) %collective-permute-start.10) | collective-permute-done | bytes 1048608 | tf_op jit(solution)/shard_map/ppermute | solution.py:375
  122.7 1.9 collective-permute-start.11
  124.6 3.4 %collective-permute-start.8 = (bf16[256,2048]{1,0:T(8,128)(2,1)}, bf16[256,2048]{1,0:T(8,128)(2,1)}, u32[]{:S(2)}, u32[]{:S(2)}) collective-permute-start(bf16[256,2048]{1,0:T(8,128)(2,1)} %collective-permute-done.7.rest_1_), channel_id=1, source_target_pairs={{4,0},{6,2},{8,4},{10,6},{12,8},{14,10},{5,1},{7,3},{9,5},{11,7},{... | collective-permute-start | bytes 3145736 | tf_op jit(solution)/shard_map/ppermute | solution.py:375
  128.1 13.6 %collective-permute-done.21.rest_0_ = bf16[256,2048]{1,0:T(8,128)(2,1)S(1)} collective-permute-done((bf16[256,2048]{1,0:T(8,128)(2,1)S(1)}, bf16[256,2048]{1,0:T(8,128)(2,1)S(1)}, u32[]{:S(2)}, u32[]{:S(2)}) %collective-permute-start.21) | collective-permute-done | bytes 1048608 | tf_op jit(solution)/shard_map/ppermute | solution.py:375
  141.7 4.3 %collective-permute-start.22 = (bf16[256,2048]{1,0:T(8,128)(2,1)S(1)}, bf16[256,2048]{1,0:T(8,128)(2,1)S(1)}, u32[]{:S(2)}, u32[]{:S(2)}) collective-permute-start(bf16[256,2048]{1,0:T(8,128)(2,1)S(1)} %collective-permute-done.21.rest_0_), channel_id=1, source_target_pairs={{4,0},{6,2},{8,4},{10,6},{12,8},{14,10},{5,1},{7,3},{9,5},{11,7},{... | collective-permute-start | bytes 3145736 | tf_op jit(solution)/shard_map/ppermute | solution.py:375
  146.0 1.9 collective-permute-start.25
  147.9 19.6 %collective-permute-done.11.rest_3_ = bf16[256,2048]{1,0:T(8,128)(2,1)S(1)} collective-permute-done((bf16[256,2048]{1,0:T(8,128)(2,1)}, bf16[256,2048]{1,0:T(8,128)(2,1)S(1)}, u32[]{:S(2)}, u32[]{:S(2)}) %collective-permute-start.11) | collective-permute-done | bytes 1048608 | tf_op jit(solution)/shard_map/ppermute | solution.py:375
  167.5 1.9 collective-permute-start.12
  169.5 3.4 %collective-permute-start.9 = (bf16[256,2048]{1,0:T(8,128)(2,1)}, bf16[256,2048]{1,0:T(8,128)(2,1)S(1)}, u32[]{:S(2)}, u32[]{:S(2)}) collective-permute-start(bf16[256,2048]{1,0:T(8,128)(2,1)} %collective-permute-done.8.rest_1_), channel_id=1, source_target_pairs={{4,0},{6,2},{8,4},{10,6},{12,8},{14,10},{5,1},{7,3},{9,5},{11,7},{... | collective-permute-start | bytes 3145736 | tf_op jit(solution)/shard_map/ppermute | solution.py:375
  172.9 16.0 %shard_map.67 = (bf16[256,2048]{1,0:T(8,128)(2,1)S(1)}, bf16[256,2048]{1,0:T(8,128)(2,1)S(1)}) custom-call(s32[2]{0:T(128)S(1)} %pad_add_fusion.1.meta, bf16[256,2048]{1,0:T(8,128)(2,1)S(1)} %collective-permute-done.20.rest_0_, bf16[256,2048]{1,0:T(8,128)(2,1)} %collective-permute-done.7.rest_1_, bf16[256,2048]{1,0:T(8,128)(2,1)} %collective-permute-done.23.rest_2_, ...), custom_call_target="tpu_custom_call" | custom-call | flops 8589934592 | bytes 16777216 | tf_op jit(solution)/shard_map/pallas_call | solution.py:241
  190.1 3.4 %copy-done.1 = bf16[4096,1024]{1,0:T(8,128)(2,1)S(1)} copy-done((bf16[4096,1024]{1,0:T(8,128)(2,1)S(1)}, bf16[4096,1024]{1,0:T(8,128)(2,1)}, u32[]{:S(2)}) %copy-start.1) | copy-done | bytes 8388632
  193.5 9.6 %shard_map.69 = bf16[256,2048]{1,0:T(8,128)(2,1)S(1)} custom-call(s32[2]{0:T(128)S(1)} %broadcast_1_meta.2.meta, bf16[256,2048]{1,0:T(8,128)(2,1)S(1)} %copy-done.5, bf16[256,2048]{1,0:T(8,128)(2,1)S(1)} %copy-done.6, bf16[4096,1024]{1,0:T(8,128)(2,1)S(1)} %copy-done.1, bf16[4096,1024]{1,0:T(8,128)(2,1)} %collective-permute-done.26.rest_3_.rest_5_), custom_call_target="tpu_custom_call" | custom-call | flops 4294967296 | bytes 16777216 | tf_op jit(solution)/shard_map/pallas_call | solution.py:241
  203.2 2.4 collective-permute-start.41
  205.6 3.4 %copy-done.2 = bf16[4096,1024]{1,0:T(8,128)(2,1)S(1)} copy-done((bf16[4096,1024]{1,0:T(8,128)(2,1)S(1)}, bf16[4096,1024]{1,0:T(8,128)(2,1)}, u32[]{:S(2)}) %copy-start.2) | copy-done | bytes 8388632
  209.0 10.7 %shard_map.68 = (bf16[128,2048]{1,0:T(8,128)(2,1)S(1)}, bf16[128,2048]{1,0:T(8,128)(2,1)S(1)}) custom-call(s32[2]{0:T(128)S(1)} %pad_add_fusion.1.meta, bf16[256,2048]{1,0:T(8,128)(2,1)S(1)} %collective-permute-done.21.rest_0_, bf16[256,2048]{1,0:T(8,128)(2,1)} %collective-permute-done.8.rest_1_, bf16[256,2048]{1,0:T(8,128)(2,1)} %collective-permute-done.24.rest_2_, ...), custom_call_target="tpu_custom_call" | custom-call | flops 4294967296 | bytes 16777216 | tf_op jit(solution)/shard_map/pallas_call | solution.py:241
  219.7 3.4 %copy-done.3 = bf16[4096,1024]{1,0:T(8,128)(2,1)S(1)} copy-done((bf16[4096,1024]{1,0:T(8,128)(2,1)S(1)}, bf16[4096,1024]{1,0:T(8,128)(2,1)}, u32[]{:S(2)}) %copy-start.3) | copy-done | bytes 8388632
  223.1 6.3 %shard_map.64.rest_2_ = f32[256,2048]{1,0:T(8,128)S(1)} custom-call(s32[2]{0:T(128)S(1)} %pad_add_fusion.1.meta, bf16[256,2048]{1,0:T(8,128)(2,1)S(1)} %collective-permute-done.22.rest_0_, bf16[256,2048]{1,0:T(8,128)(2,1)S(1)} %collective-permute-done.25.rest_1_, bf16[4096,1024]{1,0:T(8,128)(2,1)S(1)} %copy-done.3, ...), custom_call_target="tpu_custom_call" | custom-call | flops 2147483648 | bytes 8388608 | tf_op jit(solution)/shard_map/pallas_call | solution.py:241
  229.4 3.8 %shard_map.66 = (bf16[128,1024]{1,0:T(8,128)(2,1)S(1)}, bf16[128,1024]{1,0:T(8,128)(2,1)S(1)}) custom-call(s32[2]{0:T(128)S(1)} %pad_add_fusion.1.meta, bf16[256,2048]{1,0:T(8,128)(2,1)S(1)} %collective-permute-done.9.rest_0_, bf16[256,2048]{1,0:T(8,128)(2,1)S(1)} %collective-permute-done.12.rest_1_, f32[256,2048]{1,0:T(8,128)S(1)} %shard_map.64.rest_2_, ...), custom_call_target="tpu_custom_call" | custom-call | flops 1073741824 | bytes 4194304 | tf_op jit(solution)/shard_map/pallas_call | solution.py:241
  233.2 1.5 collective-permute-start.30
  234.7 3.4 %copy-done.4 = bf16[4096,1024]{1,0:T(8,128)(2,1)S(1)} copy-done((bf16[4096,1024]{1,0:T(8,128)(2,1)S(1)}, bf16[4096,1024]{1,0:T(8,128)(2,1)}, u32[]{:S(2)}) %copy-start.4) | copy-done | bytes 8388632
  238.1 2.5 shard_map.65
  240.7 6.0 %collective-permute-done.38 = bf16[128,2048]{1,0:T(8,128)(2,1)S(1)} collective-permute-done((bf16[128,2048]{1,0:T(8,128)(2,1)S(1)}, bf16[128,2048]{1,0:T(8,128)(2,1)S(1)}, u32[]{:S(2)}, u32[]{:S(2)}) %collective-permute-start.38) | collective-permute-done | bytes 524320 | tf_op jit(solution)/shard_map/ppermute | solution.py:383
  248.2 1.9 collective-permute-start.40
  253.7 2.1 collective-permute-done.27
  255.8 1.9 collective-permute-start.35
  257.7 1.5 collective-permute-start.36
  259.2 4.2 %collective-permute-done.39.refs_4_ = bf16[128,2048]{1,0:T(8,128)(2,1)S(1)} collective-permute-done((bf16[128,2048]{1,0:T(8,128)(2,1)S(1)}, bf16[128,2048]{1,0:T(8,128)(2,1)S(1)}, u32[]{:S(2)}, u32[]{:S(2)}) %collective-permute-start.39) | collective-permute-done | bytes 524320 | tf_op jit(solution)/shard_map/ppermute | solution.py:402
  263.4 2.1 collective-permute-start.37
  266.3 3.6 %collective-permute-done.40.refs_5_ = bf16[128,2048]{1,0:T(8,128)(2,1)S(1)} collective-permute-done((bf16[128,2048]{1,0:T(8,128)(2,1)S(1)}, bf16[128,2048]{1,0:T(8,128)(2,1)S(1)}, u32[]{:S(2)}, u32[]{:S(2)}) %collective-permute-start.40) | collective-permute-done | bytes 524320 | tf_op jit(solution)/shard_map/ppermute | solution.py:403
  271.2 20.9 %collective-permute-done.34.refs_0_ = bf16[128,2048]{1,0:T(8,128)(2,1)S(1)} collective-permute-done((bf16[128,2048]{1,0:T(8,128)(2,1)S(1)}, bf16[128,2048]{1,0:T(8,128)(2,1)S(1)}, u32[]{:S(2)}, u32[]{:S(2)}) %collective-permute-start.34) | collective-permute-done | bytes 524320 | tf_op jit(solution)/shard_map/ppermute | solution.py:402
  297.4 2.6 add.32.refs_6_
  300.1 3.6 %collect.1.refs_4_ = bf16[256,4096]{1,0:T(8,128)(2,1)} custom-call(s32[3]{0:T(128)} %pad_add_fusion.meta, bf16[128,2048]{1,0:T(8,128)(2,1)} %copy-done.11, bf16[128,2048]{1,0:T(8,128)(2,1)} %copy-done.12, bf16[128,2048]{1,0:T(8,128)(2,1)} %collective-permute-done.36.refs_2_, bf16[128,2048]{1,0:T(8,128)(2,1)} %collective-permute-done.37.refs_3_, ...), custom_call_target="tpu_custom_call" | custom-call | tf_op jit(solution)/shard_map/collect/pallas_call | solution.py:337
  (119 shorter events, 25.0 us)
Async XLA Ops:
  0.0 44.2 %copy-start = (s32[16,16]{1,0:T(8,128)S(1)}, s32[16,16]{1,0:T(8,128)}, u32[]{:S(2)}) copy-start(s32[16,16]{1,0:T(8,128)} %param.10) | copy-start | bytes 3076
  0.0 172.8 %collective-permute-start.26 = (bf16[4096,1024]{1,0:T(8,128)(2,1)}, bf16[4096,1024]{1,0:T(8,128)(2,1)}, u32[]{:S(2)}, u32[]{:S(2)}) collective-permute-start(bf16[4096,1024]{1,0:T(8,128)(2,1)} %rest_2_.3), channel_id=1, source_target_pairs={{0,2},{2,0},{4,6},{6,4},{8,10},{10,8},{12,14},{14,12},{1,3},{3,1},... | collective-permute-start | bytes 25165832 | tf_op jit(solution)/shard_map/ppermute | solution.py:379
  1.8 9.7 %collective-permute-start.13 = (bf16[256,512]{1,0:T(8,128)(2,1)S(1)}, bf16[256,512]{1,0:T(8,128)(2,1)S(1)}, u32[]{:S(2)}, u32[]{:S(2)}) collective-permute-start(bf16[256,512]{1,0:T(8,128)(2,1)S(1)} %pad_maximum_fusion.1.rest_0_), channel_id=1, source_target_pairs={{0,4},{2,6},{4,8},{6,10},{8,12},{10,14},{1,5},{3,7},{5,9},{7,11},{... | collective-permute-start | bytes 786440 | tf_op jit(solution)/shard_map/ppermute | solution.py:375
  5.1 11.9 %collective-permute-start.14 = (bf16[256,512]{1,0:T(8,128)(2,1)S(1)}, bf16[256,512]{1,0:T(8,128)(2,1)S(1)}, u32[]{:S(2)}, u32[]{:S(2)}) collective-permute-start(bf16[256,512]{1,0:T(8,128)(2,1)S(1)} %pad_maximum_fusion.1.rest_0_), channel_id=1, source_target_pairs={{0,8},{2,10},{4,12},{6,14},{1,9},{3,11},{5,13},{7,15},{16,24},{18,... | collective-permute-start | bytes 786440 | tf_op jit(solution)/shard_map/ppermute | solution.py:375
  6.4 13.4 %collective-permute-start.15 = (bf16[256,512]{1,0:T(8,128)(2,1)S(1)}, bf16[256,512]{1,0:T(8,128)(2,1)S(1)}, u32[]{:S(2)}, u32[]{:S(2)}) collective-permute-start(bf16[256,512]{1,0:T(8,128)(2,1)S(1)} %pad_maximum_fusion.1.rest_0_), channel_id=1, source_target_pairs={{0,12},{2,14},{1,13},{3,15},{16,28},{18,30},{17,29},{19,31}} | collective-permute-start | bytes 786440 | tf_op jit(solution)/shard_map/ppermute | solution.py:375
  7.0 13.5 %collective-permute-start.16 = (bf16[256,512]{1,0:T(8,128)(2,1)S(1)}, bf16[256,512]{1,0:T(8,128)(2,1)S(1)}, u32[]{:S(2)}, u32[]{:S(2)}) collective-permute-start(bf16[256,512]{1,0:T(8,128)(2,1)S(1)} %pad_maximum_fusion.1.rest_0_), channel_id=1, source_target_pairs={{0,2},{2,0},{4,6},{6,4},{8,10},{10,8},{12,14},{14,12},{1,3},{3,1},... | collective-permute-start | bytes 786440 | tf_op jit(solution)/shard_map/ppermute | solution.py:379
  7.6 38.0 %copy-start.13 = (bf16[256,512]{1,0:T(8,128)(2,1)}, bf16[256,512]{1,0:T(8,128)(2,1)S(1)}, u32[]{:S(2)}) copy-start(bf16[256,512]{1,0:T(8,128)(2,1)S(1)} %pad_maximum_fusion.rest_0_) | copy-start | bytes 786436
  11.6 28.1 %collective-permute-start = (bf16[256,512]{1,0:T(8,128)(2,1)S(1)}, bf16[256,512]{1,0:T(8,128)(2,1)S(1)}, u32[]{:S(2)}, u32[]{:S(2)}) collective-permute-start(bf16[256,512]{1,0:T(8,128)(2,1)S(1)} %pad_maximum_fusion.rest_0_), channel_id=1, source_target_pairs={{0,4},{2,6},{4,8},{6,10},{8,12},{10,14},{1,5},{3,7},{5,9},{7,11},{... | collective-permute-start | bytes 786440 | tf_op jit(solution)/shard_map/ppermute | solution.py:375
  17.0 27.1 %collective-permute-start.1 = (bf16[256,512]{1,0:T(8,128)(2,1)S(1)}, bf16[256,512]{1,0:T(8,128)(2,1)S(1)}, u32[]{:S(2)}, u32[]{:S(2)}) collective-permute-start(bf16[256,512]{1,0:T(8,128)(2,1)S(1)} %pad_maximum_fusion.rest_0_), channel_id=1, source_target_pairs={{0,8},{2,10},{4,12},{6,14},{1,9},{3,11},{5,13},{7,15},{16,24},{18,... | collective-permute-start | bytes 786440 | tf_op jit(solution)/shard_map/ppermute | solution.py:375
  19.8 25.8 %collective-permute-start.2 = (bf16[256,512]{1,0:T(8,128)(2,1)S(1)}, bf16[256,512]{1,0:T(8,128)(2,1)S(1)}, u32[]{:S(2)}, u32[]{:S(2)}) collective-permute-start(bf16[256,512]{1,0:T(8,128)(2,1)S(1)} %pad_maximum_fusion.rest_0_), channel_id=1, source_target_pairs={{0,12},{2,14},{1,13},{3,15},{16,28},{18,30},{17,29},{19,31}} | collective-permute-start | bytes 786440 | tf_op jit(solution)/shard_map/ppermute | solution.py:375
  20.5 25.5 %collective-permute-start.17 = (bf16[256,512]{1,0:T(8,128)(2,1)S(1)}, bf16[256,512]{1,0:T(8,128)(2,1)S(1)}, u32[]{:S(2)}, u32[]{:S(2)}) collective-permute-start(bf16[256,512]{1,0:T(8,128)(2,1)S(1)} %collective-permute-done.13.rest_1_), channel_id=1, source_target_pairs={{0,2},{2,0},{4,6},{6,4},{8,10},{10,8},{12,14},{14,12},{1,3},{3,1},... | collective-permute-start | bytes 786440 | tf_op jit(solution)/shard_map/ppermute | solution.py:379
  39.6 6.5 %collective-permute-start.18 = (bf16[256,512]{1,0:T(8,128)(2,1)S(1)}, bf16[256,512]{1,0:T(8,128)(2,1)}, u32[]{:S(2)}, u32[]{:S(2)}) collective-permute-start(bf16[256,512]{1,0:T(8,128)(2,1)S(1)} %collective-permute-done.14.rest_2_), channel_id=1, source_target_pairs={{0,2},{2,0},{4,6},{6,4},{8,10},{10,8},{12,14},{14,12},{1,3},{3,1},... | collective-permute-start | bytes 786440 | tf_op jit(solution)/shard_map/ppermute | solution.py:379
  44.1 2.5 collective-permute-start.19
  45.6 14.4 %collective-permute-start.3 = (bf16[256,512]{1,0:T(8,128)(2,1)S(1)}, bf16[256,512]{1,0:T(8,128)(2,1)S(1)}, u32[]{:S(2)}, u32[]{:S(2)}) collective-permute-start(bf16[256,512]{1,0:T(8,128)(2,1)S(1)} %pad_maximum_fusion.rest_0_), channel_id=1, source_target_pairs={{0,2},{2,0},{4,6},{6,4},{8,10},{10,8},{12,14},{14,12},{1,3},{3,1},... | collective-permute-start | bytes 786440 | tf_op jit(solution)/shard_map/ppermute | solution.py:379
  46.0 26.8 %collective-permute-start.4 = (bf16[256,512]{1,0:T(8,128)(2,1)S(1)}, bf16[256,512]{1,0:T(8,128)(2,1)S(1)}, u32[]{:S(2)}, u32[]{:S(2)}) collective-permute-start(bf16[256,512]{1,0:T(8,128)(2,1)S(1)} %collective-permute-done.rest_1_), channel_id=1, source_target_pairs={{0,2},{2,0},{4,6},{6,4},{8,10},{10,8},{12,14},{14,12},{1,3},{3,1},... | collective-permute-start | bytes 786440 | tf_op jit(solution)/shard_map/ppermute | solution.py:379
  46.1 28.7 %collective-permute-start.5 = (bf16[256,512]{1,0:T(8,128)(2,1)S(1)}, bf16[256,512]{1,0:T(8,128)(2,1)}, u32[]{:S(2)}, u32[]{:S(2)}) collective-permute-start(bf16[256,512]{1,0:T(8,128)(2,1)S(1)} %collective-permute-done.1.rest_2_), channel_id=1, source_target_pairs={{0,2},{2,0},{4,6},{6,4},{8,10},{10,8},{12,14},{14,12},{1,3},{3,1},... | collective-permute-start | bytes 786440 | tf_op jit(solution)/shard_map/ppermute | solution.py:379
  46.6 28.2 %collective-permute-start.6 = (bf16[256,512]{1,0:T(8,128)(2,1)S(1)}, bf16[256,512]{1,0:T(8,128)(2,1)}, u32[]{:S(2)}, u32[]{:S(2)}) collective-permute-start(bf16[256,512]{1,0:T(8,128)(2,1)S(1)} %collective-permute-done.2.rest_3_), channel_id=1, source_target_pairs={{0,2},{2,0},{4,6},{6,4},{8,10},{10,8},{12,14},{14,12},{1,3},{3,1},... | collective-permute-start | bytes 786440 | tf_op jit(solution)/shard_map/ppermute | solution.py:379
  60.0 36.0 %collective-permute-start.20 = (bf16[256,2048]{1,0:T(8,128)(2,1)}, bf16[256,2048]{1,0:T(8,128)(2,1)S(1)}, u32[]{:S(2)}, u32[]{:S(2)}) collective-permute-start(bf16[256,2048]{1,0:T(8,128)(2,1)} %attend.3.rest_0_), channel_id=1, source_target_pairs={{4,0},{6,2},{8,4},{10,6},{12,8},{14,10},{5,1},{7,3},{9,5},{11,7},{... | collective-permute-start | bytes 3145736 | tf_op jit(solution)/shard_map/ppermute | solution.py:375
  72.9 27.6 %collective-permute-start.23 = (bf16[256,2048]{1,0:T(8,128)(2,1)}, bf16[256,2048]{1,0:T(8,128)(2,1)}, u32[]{:S(2)}, u32[]{:S(2)}) collective-permute-start(bf16[256,2048]{1,0:T(8,128)(2,1)} %attend.3.rest_0_), channel_id=1, source_target_pairs={{0,4},{2,6},{4,8},{6,10},{8,12},{10,14},{1,5},{3,7},{5,9},{7,11},{... | collective-permute-start | bytes 3145736 | tf_op jit(solution)/shard_map/ppermute | solution.py:375
  86.8 35.9 %collective-permute-start.10 = (bf16[256,2048]{1,0:T(8,128)(2,1)}, bf16[256,2048]{1,0:T(8,128)(2,1)}, u32[]{:S(2)}, u32[]{:S(2)}) collective-permute-start(bf16[256,2048]{1,0:T(8,128)(2,1)} %attend.2.rest_1_), channel_id=1, source_target_pairs={{0,4},{2,6},{4,8},{6,10},{8,12},{10,14},{1,5},{3,7},{5,9},{7,11},{... | collective-permute-start | bytes 3145736 | tf_op jit(solution)/shard_map/ppermute | solution.py:375
  88.8 35.9 %collective-permute-start.7 = (bf16[256,2048]{1,0:T(8,128)(2,1)}, bf16[256,2048]{1,0:T(8,128)(2,1)}, u32[]{:S(2)}, u32[]{:S(2)}) collective-permute-start(bf16[256,2048]{1,0:T(8,128)(2,1)} %attend.2.rest_1_), channel_id=1, source_target_pairs={{4,0},{6,2},{8,4},{10,6},{12,8},{14,10},{5,1},{7,3},{9,5},{11,7},{... | collective-permute-start | bytes 3145736 | tf_op jit(solution)/shard_map/ppermute | solution.py:375
  96.0 45.6 %collective-permute-start.21 = (bf16[256,2048]{1,0:T(8,128)(2,1)S(1)}, bf16[256,2048]{1,0:T(8,128)(2,1)S(1)}, u32[]{:S(2)}, u32[]{:S(2)}) collective-permute-start(bf16[256,2048]{1,0:T(8,128)(2,1)S(1)} %collective-permute-done.20.rest_0_), channel_id=1, source_target_pairs={{4,0},{6,2},{8,4},{10,6},{12,8},{14,10},{5,1},{7,3},{9,5},{11,7},{... | collective-permute-start | bytes 3145736 | tf_op jit(solution)/shard_map/ppermute | solution.py:375
  100.4 45.6 %collective-permute-start.24 = (bf16[256,2048]{1,0:T(8,128)(2,1)}, bf16[256,2048]{1,0:T(8,128)(2,1)}, u32[]{:S(2)}, u32[]{:S(2)}) collective-permute-start(bf16[256,2048]{1,0:T(8,128)(2,1)} %collective-permute-done.23.rest_2_), channel_id=1, source_target_pairs={{0,4},{2,6},{4,8},{6,10},{8,12},{10,14},{1,5},{3,7},{5,9},{7,11},{... | collective-permute-start | bytes 3145736 | tf_op jit(solution)/shard_map/ppermute | solution.py:375
  122.7 44.8 %collective-permute-start.11 = (bf16[256,2048]{1,0:T(8,128)(2,1)}, bf16[256,2048]{1,0:T(8,128)(2,1)S(1)}, u32[]{:S(2)}, u32[]{:S(2)}) collective-permute-start(bf16[256,2048]{1,0:T(8,128)(2,1)} %collective-permute-done.10.rest_3_), channel_id=1, source_target_pairs={{0,4},{2,6},{4,8},{6,10},{8,12},{10,14},{1,5},{3,7},{5,9},{7,11},{... | collective-permute-start | bytes 3145736 | tf_op jit(solution)/shard_map/ppermute | solution.py:375
  124.6 44.8 %collective-permute-start.8 = (bf16[256,2048]{1,0:T(8,128)(2,1)}, bf16[256,2048]{1,0:T(8,128)(2,1)}, u32[]{:S(2)}, u32[]{:S(2)}) collective-permute-start(bf16[256,2048]{1,0:T(8,128)(2,1)} %collective-permute-done.7.rest_1_), channel_id=1, source_target_pairs={{4,0},{6,2},{8,4},{10,6},{12,8},{14,10},{5,1},{7,3},{9,5},{11,7},{... | collective-permute-start | bytes 3145736 | tf_op jit(solution)/shard_map/ppermute | solution.py:375
  128.1 62.0 %copy-start.5 = (bf16[256,2048]{1,0:T(8,128)(2,1)S(1)}, bf16[256,2048]{1,0:T(8,128)(2,1)}, u32[]{:S(2)}) copy-start(bf16[256,2048]{1,0:T(8,128)(2,1)} %attend.3.rest_0_) | copy-start | bytes 3145732
  128.1 62.0 %copy-start.6 = (bf16[256,2048]{1,0:T(8,128)(2,1)S(1)}, bf16[256,2048]{1,0:T(8,128)(2,1)}, u32[]{:S(2)}) copy-start(bf16[256,2048]{1,0:T(8,128)(2,1)} %attend.2.rest_1_) | copy-start | bytes 3145732
  141.7 61.5 %collective-permute-start.22 = (bf16[256,2048]{1,0:T(8,128)(2,1)S(1)}, bf16[256,2048]{1,0:T(8,128)(2,1)S(1)}, u32[]{:S(2)}, u32[]{:S(2)}) collective-permute-start(bf16[256,2048]{1,0:T(8,128)(2,1)S(1)} %collective-permute-done.21.rest_0_), channel_id=1, source_target_pairs={{4,0},{6,2},{8,4},{10,6},{12,8},{14,10},{5,1},{7,3},{9,5},{11,7},{... | collective-permute-start | bytes 3145736 | tf_op jit(solution)/shard_map/ppermute | solution.py:375
  146.0 73.6 %collective-permute-start.25 = (bf16[256,2048]{1,0:T(8,128)(2,1)}, bf16[256,2048]{1,0:T(8,128)(2,1)S(1)}, u32[]{:S(2)}, u32[]{:S(2)}) collective-permute-start(bf16[256,2048]{1,0:T(8,128)(2,1)} %collective-permute-done.24.rest_2_), channel_id=1, source_target_pairs={{0,4},{2,6},{4,8},{6,10},{8,12},{10,14},{1,5},{3,7},{5,9},{7,11},{... | collective-permute-start | bytes 3145736 | tf_op jit(solution)/shard_map/ppermute | solution.py:375
  167.5 61.9 %collective-permute-start.12 = (bf16[256,2048]{1,0:T(8,128)(2,1)S(1)}, bf16[256,2048]{1,0:T(8,128)(2,1)S(1)}, u32[]{:S(2)}, u32[]{:S(2)}) collective-permute-start(bf16[256,2048]{1,0:T(8,128)(2,1)S(1)} %collective-permute-done.11.rest_3_), channel_id=1, source_target_pairs={{0,4},{2,6},{4,8},{6,10},{8,12},{10,14},{1,5},{3,7},{5,9},{7,11},{... | collective-permute-start | bytes 3145736 | tf_op jit(solution)/shard_map/ppermute | solution.py:375
  169.5 59.9 %collective-permute-start.9 = (bf16[256,2048]{1,0:T(8,128)(2,1)}, bf16[256,2048]{1,0:T(8,128)(2,1)S(1)}, u32[]{:S(2)}, u32[]{:S(2)}) collective-permute-start(bf16[256,2048]{1,0:T(8,128)(2,1)} %collective-permute-done.8.rest_1_), channel_id=1, source_target_pairs={{4,0},{6,2},{8,4},{10,6},{12,8},{14,10},{5,1},{7,3},{9,5},{11,7},{... | collective-permute-start | bytes 3145736 | tf_op jit(solution)/shard_map/ppermute | solution.py:375
  188.8 59.4 %collective-permute-start.33 = (bf16[256,2048]{1,0:T(8,128)(2,1)S(1)}, bf16[256,2048]{1,0:T(8,128)(2,1)S(1)}, u32[]{:S(2)}, u32[]{:S(2)}) collective-permute-start(bf16[256,2048]{1,0:T(8,128)(2,1)S(1)} %get-tuple-element.18), channel_id=1, source_target_pairs={{0,1},{1,0},{2,3},{3,2},{4,5},{5,4},{6,7},{7,6},{8,9},{9,8},{10,11... | collective-permute-start | bytes 3145736 | tf_op jit(solution)/shard_map/ppermute | solution.py:383
  203.2 54.5 %collective-permute-start.41 = (bf16[256,2048]{1,0:T(8,128)(2,1)S(1)}, bf16[256,2048]{1,0:T(8,128)(2,1)S(1)}, u32[]{:S(2)}, u32[]{:S(2)}) collective-permute-start(bf16[256,2048]{1,0:T(8,128)(2,1)S(1)} %shard_map.69), channel_id=1, source_target_pairs={{1,0},{3,2},{5,4},{7,6},{8,9},{10,11},{12,13},{14,15},{17,16},{19,... | collective-permute-start | bytes 3145736 | tf_op jit(solution)/shard_map/ppermute | solution.py:443
  219.7 27.1 %collective-permute-start.38 = (bf16[128,2048]{1,0:T(8,128)(2,1)S(1)}, bf16[128,2048]{1,0:T(8,128)(2,1)S(1)}, u32[]{:S(2)}, u32[]{:S(2)}) collective-permute-start(bf16[128,2048]{1,0:T(8,128)(2,1)S(1)} %get-tuple-element.20), channel_id=1, source_target_pairs={{0,1},{1,0},{2,3},{3,2},{4,5},{5,4},{6,7},{7,6},{8,9},{9,8},{10,11... | collective-permute-start | bytes 1572872 | tf_op jit(solution)/shard_map/ppermute | solution.py:383
  233.2 19.2 %collective-permute-start.30 = (bf16[128,1024]{1,0:T(8,128)(2,1)S(1)}, bf16[128,1024]{1,0:T(8,128)(2,1)S(1)}, u32[]{:S(2)}, u32[]{:S(2)}) collective-permute-start(bf16[128,1024]{1,0:T(8,128)(2,1)S(1)} %get-tuple-element.16), channel_id=1, source_target_pairs={{0,1},{1,0},{2,3},{3,2},{4,5},{5,4},{6,7},{7,6},{8,9},{9,8},{10,11... | collective-permute-start | bytes 786440 | tf_op jit(solution)/shard_map/ppermute | solution.py:383
  240.7 15.1 %collective-permute-start.27 = (bf16[128,1024]{1,0:T(8,128)(2,1)S(1)}, bf16[128,1024]{1,0:T(8,128)(2,1)S(1)}, u32[]{:S(2)}, u32[]{:S(2)}) collective-permute-start(bf16[128,1024]{1,0:T(8,128)(2,1)S(1)} %get-tuple-element.14), channel_id=1, source_target_pairs={{0,1},{1,0},{2,3},{3,2},{4,5},{5,4},{6,7},{7,6},{8,9},{9,8},{10,11... | collective-permute-start | bytes 786440 | tf_op jit(solution)/shard_map/ppermute | solution.py:383
  246.9 16.4 %collective-permute-start.39 = (bf16[128,2048]{1,0:T(8,128)(2,1)S(1)}, bf16[128,2048]{1,0:T(8,128)(2,1)S(1)}, u32[]{:S(2)}, u32[]{:S(2)}) collective-permute-start(bf16[128,2048]{1,0:T(8,128)(2,1)S(1)} %add.31), channel_id=1, source_target_pairs={{0,8},{2,10},{4,12},{6,14},{9,1},{11,3},{13,5},{15,7},{16,24},{18,... | collective-permute-start | bytes 1572872 | tf_op jit(solution)/shard_map/ppermute | solution.py:402
  248.2 21.7 %collective-permute-start.40 = (bf16[128,2048]{1,0:T(8,128)(2,1)S(1)}, bf16[128,2048]{1,0:T(8,128)(2,1)S(1)}, u32[]{:S(2)}, u32[]{:S(2)}) collective-permute-start(bf16[128,2048]{1,0:T(8,128)(2,1)S(1)} %add.31), channel_id=1, source_target_pairs={{1,8},{3,10},{5,12},{7,14},{8,1},{10,3},{12,5},{14,7},{17,24},{19,... | collective-permute-start | bytes 1572872 | tf_op jit(solution)/shard_map/ppermute | solution.py:403
  252.4 39.7 %collective-permute-start.34 = (bf16[128,2048]{1,0:T(8,128)(2,1)S(1)}, bf16[128,2048]{1,0:T(8,128)(2,1)S(1)}, u32[]{:S(2)}, u32[]{:S(2)}) collective-permute-start(bf16[128,2048]{1,0:T(8,128)(2,1)S(1)} %get-tuple-element.24), channel_id=1, source_target_pairs={{0,4},{2,6},{4,8},{6,10},{9,5},{11,7},{13,9},{15,11},{16,20},{18,2... | collective-permute-start | bytes 1572872 | tf_op jit(solution)/shard_map/ppermute | solution.py:402
  255.8 38.2 %collective-permute-start.35 = (bf16[128,2048]{1,0:T(8,128)(2,1)S(1)}, bf16[128,2048]{1,0:T(8,128)(2,1)S(1)}, u32[]{:S(2)}, u32[]{:S(2)}) collective-permute-start(bf16[128,2048]{1,0:T(8,128)(2,1)S(1)} %get-tuple-element.24), channel_id=1, source_target_pairs={{1,4},{3,6},{5,8},{7,10},{8,5},{10,7},{12,9},{14,11},{17,20},{19,2... | collective-permute-start | bytes 1572872 | tf_op jit(solution)/shard_map/ppermute | solution.py:403
  257.7 37.7 %collective-permute-start.36 = (bf16[128,2048]{1,0:T(8,128)(2,1)}, bf16[128,2048]{1,0:T(8,128)(2,1)}, u32[]{:S(2)}, u32[]{:S(2)}) collective-permute-start(bf16[128,2048]{1,0:T(8,128)(2,1)} %get-tuple-element.23), channel_id=1, source_target_pairs={{4,0},{6,2},{9,13},{11,15},{20,16},{22,18},{25,29},{27,31}} | collective-permute-start | bytes 1572872 | tf_op jit(solution)/shard_map/ppermute | solution.py:402
  263.4 36.7 %copy-start.9 = (bf16[128,2048]{1,0:T(8,128)(2,1)}, bf16[128,2048]{1,0:T(8,128)(2,1)S(1)}, u32[]{:S(2)}) copy-start(bf16[128,2048]{1,0:T(8,128)(2,1)S(1)} %collective-permute-done.39.refs_4_) | copy-start | bytes 1572868
  263.4 36.7 %collective-permute-start.37 = (bf16[128,2048]{1,0:T(8,128)(2,1)}, bf16[128,2048]{1,0:T(8,128)(2,1)}, u32[]{:S(2)}, u32[]{:S(2)}) collective-permute-start(bf16[128,2048]{1,0:T(8,128)(2,1)} %get-tuple-element.23), channel_id=1, source_target_pairs={{5,0},{7,2},{8,13},{10,15},{21,16},{23,18},{24,29},{26,31}} | collective-permute-start | bytes 1572872 | tf_op jit(solution)/shard_map/ppermute | solution.py:403
  269.9 30.1 %copy-start.10 = (bf16[128,2048]{1,0:T(8,128)(2,1)}, bf16[128,2048]{1,0:T(8,128)(2,1)S(1)}, u32[]{:S(2)}) copy-start(bf16[128,2048]{1,0:T(8,128)(2,1)S(1)} %collective-permute-done.40.refs_5_) | copy-start | bytes 1572868
  269.9 33.8 %collective-permute-start.31 = (bf16[128,1024]{1,0:T(8,128)(2,1)}, bf16[128,1024]{1,0:T(8,128)(2,1)}, u32[]{:S(2)}, u32[]{:S(2)}) collective-permute-start(bf16[128,1024]{1,0:T(8,128)(2,1)} %add.29), channel_id=1, source_target_pairs={{0,12},{2,14},{13,1},{15,3},{16,28},{18,30},{29,17},{31,19}} | collective-permute-start | bytes 786440 | tf_op jit(solution)/shard_map/ppermute | solution.py:402
  292.1 11.5 %collective-permute-start.32 = (bf16[128,1024]{1,0:T(8,128)(2,1)}, bf16[128,1024]{1,0:T(8,128)(2,1)}, u32[]{:S(2)}, u32[]{:S(2)}) collective-permute-start(bf16[128,1024]{1,0:T(8,128)(2,1)} %add.29), channel_id=1, source_target_pairs={{1,12},{3,14},{12,1},{14,3},{17,28},{19,30},{28,17},{30,19}} | collective-permute-start | bytes 786440 | tf_op jit(solution)/shard_map/ppermute | solution.py:403
  294.0 9.6 %collective-permute-start.28 = (bf16[128,1024]{1,0:T(8,128)(2,1)S(1)}, bf16[128,1024]{1,0:T(8,128)(2,1)}, u32[]{:S(2)}, u32[]{:S(2)}) collective-permute-start(bf16[128,1024]{1,0:T(8,128)(2,1)S(1)} %add.28), channel_id=1, source_target_pairs={{0,12},{2,14},{13,1},{15,3},{16,28},{18,30},{29,17},{31,19}} | collective-permute-start | bytes 786440 | tf_op jit(solution)/shard_map/ppermute | solution.py:402
  295.4 8.3 %collective-permute-start.29 = (bf16[128,1024]{1,0:T(8,128)(2,1)S(1)}, bf16[128,1024]{1,0:T(8,128)(2,1)}, u32[]{:S(2)}, u32[]{:S(2)}) collective-permute-start(bf16[128,1024]{1,0:T(8,128)(2,1)S(1)} %add.28), channel_id=1, source_target_pairs={{1,12},{3,14},{12,1},{14,3},{17,28},{19,30},{28,17},{30,19}} | collective-permute-start | bytes 786440 | tf_op jit(solution)/shard_map/ppermute | solution.py:403
  (20 other events, 241.1 us)
where the time goes:
time: 306 us; the launch traced here: 305 us
  waiting for transfers between devices  108 us (35%)
  starting transfers between devices  94 us (31%)
  Pallas kernels  77.2 us (25%)
  local copies, waits for them, and re-layouts  19.3 us (6%)
  other arithmetic  5.32 us (2%)
    ppermute x18, waiting for transfers between devices, line(): return lax.ppermute(x, 'ctx', pairs)  69.6 us
    ppermute x18, starting transfers between devices, line(): return lax.ppermute(x, 'ctx', pairs)  57.2 us
    pallas_call x6, Pallas kernels, project(): pl.pallas_call(functools.partial(project_body, mode, tiles, len(a), bool(...  48.9 us
    ppermute x5, waiting for transfers between devices, send_back(): one = lax.ppermute(total, LANES, straight)  25.1 us
    pallas_call x2, Pallas kernels, attention(): pl.pallas_call(functools.partial(attn_body, cores, skip), grid_spec=grid_...  24 us
    ppermute x9, starting transfers between devices, partner(): lax.ppermute(x, 'ctx', [(i, i ^ 1) for i in range(lax.axis_size('ctx'))])  16.1 us
    unnamed x52, local copies, waits for them, and re-layouts  13.6 us
    ppermute x4, waiting for transfers between devices, across(): return lax.ppermute(x, 'heads', [(0, 1), (1, 0)])  9.07 us
  transfers between devices with their start and end apart: 42, of which 13 were waited for; matrix products, arithmetic and copies ran while one was open for 4% of the time, Pallas kernels for 25%

commit v1 on v0

--- a/solution.py
+++ b/solution.py
@@ -307,22 +307,21 @@
 
 
 def finish_body(meta, *refs):
-    third, (_, out, held, sem) = refs[:4], refs[4:]
+    third, (_, out, held, sem) = refs[:2], refs[2:]
     chip, side, core = meta[0], meta[1], meta[2]
+    cols = out.shape[1] // 4
     for piece in range(2):
         spots = spots_of("third", piece)
 
         @pl.when(any_of(spots, chip, side))
         def _(piece=piece):
-            into = [
-                pltpu.make_async_copy(third[n], held.at[n], sem.at[n]) for n in range(4)
-            ]
-            back = [
-                pltpu.make_async_copy(
-                    held.at[n], block_at(out, core, side, piece, n // 2, n % 2), sem.at[n]
-                )
-                for n in range(4)
-            ]
+            into, back = [], []
+            for n in range(4):
+                o, r = n // 2, n % 2
+                src = third[r].at[:, pl.ds(o * cols, cols)]
+                into.append(pltpu.make_async_copy(src, held.at[n], sem.at[n]))
+                dst = block_at(out, core, side, piece, o, r)
+                back.append(pltpu.make_async_copy(held.at[n], dst, sem.at[n]))
             for copy in into:
                 copy.start()
             for one, two in zip(into, back):
@@ -359,7 +358,7 @@
             in_specs=[anywhere] * (len(arrays) + 1),
             out_specs=anywhere,
             scratch_shapes=[
-                pltpu.VMEM((4,) + arrays[0].shape, jnp.bfloat16),
+                pltpu.VMEM((4, out.shape[0] // 2, out.shape[1] // 4), jnp.bfloat16),
                 pltpu.SemaphoreType.DMA((4,)),
             ],
         ),
@@ -464,8 +463,9 @@
             row=1,
             part=(early, o * cols // 512),
         )
-        thirds += send_back("third", keep + across(send))
-    return finish(chip, side, core, thirds, out)
+        thirds.append(keep + across(send))
+    last = send_back("third", jnp.concatenate(thirds, axis=1))
+    return finish(chip, side, core, last, out)
 
 
 def gathered(queries, keys, values, doc_ids, block_mask, out_weight):

time: 306 us -> 314 us (1.026)
  the two profiles are of different devices: /device:TPU:17 before, /device:TPU:0 now
where the time goes in v1:
time: 314 us; the launch traced here: 312 us
  starting transfers between devices  122 us (39%)
  waiting for transfers between devices  85.8 us (27%)
  Pallas kernels  72.9 us (23%)
  local copies, waits for them, and re-layouts  22.5 us (7%)
  other arithmetic  7.75 us (2%)
    ppermute x18, starting transfers between devices, line(): return lax.ppermute(x, 'ctx', pairs)  92.8 us
    pallas_call x6, Pallas kernels, project(): pl.pallas_call(functools.partial(project_body, mode, tiles, len(a), bool(...  52.6 us
    ppermute x18, waiting for transfers between devices, line(): return lax.ppermute(x, 'ctx', pairs)  52.1 us
    unnamed x72, local copies, waits for them, and re-layouts  16.4 us
    ppermute x4, waiting for transfers between devices, across(): return lax.ppermute(x, 'heads', [(0, 1), (1, 0)])  16.3 us
    pallas_call x2, Pallas kernels, attention(): pl.pallas_call(functools.partial(attn_body, cores, skip), grid_spec=grid_...  15.9 us
    ppermute x4, starting transfers between devices, send_back(): one = lax.ppermute(total, LANES, straight)  15.9 us
    ppermute x4, waiting for transfers between devices, send_back(): one = lax.ppermute(total, LANES, straight)  15.1 us
  transfers between devices with their start and end apart: 40, of which 9 were waited for; matrix products, arithmetic and copies ran while one was open for 4% of the time, Pallas kernels for 23%

profile of v1, /device:TPU:0, one launch (start us, length us, event | category | flops | bytes accessed | tf_op | source)
XLA Modules:
  0.0 312.1 jit_solution(12992549358825622424)
XLA Ops:
  1.8 4.5 %collective-permute-start.13 = (bf16[256,512]{1,0:T(8,128)(2,1)S(1)}, bf16[256,512]{1,0:T(8,128)(2,1)S(1)}, u32[]{:S(2)}, u32[]{:S(2)}) collective-permute-start(bf16[256,512]{1,0:T(8,128)(2,1)S(1)} %pad_maximum_fusion.2.rest_0_), channel_id=1, source_target_pairs={{0,4},{2,6},{4,8},{6,10},{8,12},{10,14},{1,5},{3,7},{5,9},{7,11},{... | collective-permute-start | bytes 786440 | tf_op jit(solution)/shard_map/ppermute | solution.py:374
  6.3 4.5 %collective-permute-start.14 = (bf16[256,512]{1,0:T(8,128)(2,1)S(1)}, bf16[256,512]{1,0:T(8,128)(2,1)S(1)}, u32[]{:S(2)}, u32[]{:S(2)}) collective-permute-start(bf16[256,512]{1,0:T(8,128)(2,1)S(1)} %pad_maximum_fusion.2.rest_0_), channel_id=1, source_target_pairs={{0,8},{2,10},{4,12},{6,14},{1,9},{3,11},{5,13},{7,15},{16,24},{18,... | collective-permute-start | bytes 786440 | tf_op jit(solution)/shard_map/ppermute | solution.py:374
  10.8 1.3 collective-permute-start.15
  13.0 14.3 %collective-permute-start = (bf16[256,512]{1,0:T(8,128)(2,1)S(1)}, bf16[256,512]{1,0:T(8,128)(2,1)S(1)}, u32[]{:S(2)}, u32[]{:S(2)}) collective-permute-start(bf16[256,512]{1,0:T(8,128)(2,1)S(1)} %pad_maximum_fusion.1.rest_0_), channel_id=1, source_target_pairs={{0,4},{2,6},{4,8},{6,10},{8,12},{10,14},{1,5},{3,7},{5,9},{7,11},{... | collective-permute-start | bytes 786440 | tf_op jit(solution)/shard_map/ppermute | solution.py:374
  27.3 4.3 %collective-permute-start.1 = (bf16[256,512]{1,0:T(8,128)(2,1)S(1)}, bf16[256,512]{1,0:T(8,128)(2,1)S(1)}, u32[]{:S(2)}, u32[]{:S(2)}) collective-permute-start(bf16[256,512]{1,0:T(8,128)(2,1)S(1)} %pad_maximum_fusion.1.rest_0_), channel_id=1, source_target_pairs={{0,8},{2,10},{4,12},{6,14},{1,9},{3,11},{5,13},{7,15},{16,24},{18,... | collective-permute-start | bytes 786440 | tf_op jit(solution)/shard_map/ppermute | solution.py:374
  31.6 1.5 fusion
  33.1 11.5 %collective-permute-start.2 = (bf16[256,512]{1,0:T(8,128)(2,1)S(1)}, bf16[256,512]{1,0:T(8,128)(2,1)S(1)}, u32[]{:S(2)}, u32[]{:S(2)}) collective-permute-start(bf16[256,512]{1,0:T(8,128)(2,1)S(1)} %pad_maximum_fusion.1.rest_0_), channel_id=1, source_target_pairs={{0,12},{2,14},{1,13},{3,15},{16,28},{18,30},{17,29},{19,31}} | collective-permute-start | bytes 786440 | tf_op jit(solution)/shard_map/ppermute | solution.py:374
  46.9 1.6 collective-permute-done.2.rest_3_
  51.0 8.0 %attend.3.rest_0_ = bf16[256,2048]{1,0:T(8,128)(2,1)} custom-call(s32[3]{0:T(128)} %pad_add_fusion.2.meta, s32[16]{0:T(128)} %slice_reduce_fusion.dlast, s32[32]{0:T(128)} %reshape.12.links, s32[256,128]{1,0:T(8,128)} %broadcast_in_dim.16.docq, s32[16,128]{1,0:T(8,128)} %bitcast.10, bf16[256,2048]{1,0:T(8,128)(2,1)} %get-tuple-element.21.q, ...), custom_call_target="tpu_custom_call" | custom-call | flops 2147483648 | bytes 4194304 | tf_op jit(solution)/shard_map/attend/pallas_call | solution.py:134
  59.0 1.3 collective-permute-start.20
  60.4 15.2 %collective-permute-start.23 = (bf16[256,2048]{1,0:T(8,128)(2,1)}, bf16[256,2048]{1,0:T(8,128)(2,1)}, u32[]{:S(2)}, u32[]{:S(2)}) collective-permute-start(bf16[256,2048]{1,0:T(8,128)(2,1)} %attend.3.rest_0_), channel_id=1, source_target_pairs={{0,4},{2,6},{4,8},{6,10},{8,12},{10,14},{1,5},{3,7},{5,9},{7,11},{... | collective-permute-start | bytes 3145736 | tf_op jit(solution)/shard_map/ppermute | solution.py:374
  76.4 8.0 %attend.2.rest_1_ = bf16[256,2048]{1,0:T(8,128)(2,1)} custom-call(s32[3]{0:T(128)} %pad_add_fusion.2.meta, s32[16]{0:T(128)} %slice_reduce_fusion.dlast, s32[32]{0:T(128)} %reshape.12.links, s32[256,128]{1,0:T(8,128)} %broadcast_in_dim.16.docq, s32[16,128]{1,0:T(8,128)} %bitcast.11, bf16[256,2048]{1,0:T(8,128)(2,1)} %get-tuple-element.22.q, ...), custom_call_target="tpu_custom_call" | custom-call | flops 2147483648 | bytes 4194304 | tf_op jit(solution)/shard_map/attend/pallas_call | solution.py:134
  84.4 9.2 %collective-permute-start.10 = (bf16[256,2048]{1,0:T(8,128)(2,1)}, bf16[256,2048]{1,0:T(8,128)(2,1)}, u32[]{:S(2)}, u32[]{:S(2)}) collective-permute-start(bf16[256,2048]{1,0:T(8,128)(2,1)} %attend.2.rest_1_), channel_id=1, source_target_pairs={{0,4},{2,6},{4,8},{6,10},{8,12},{10,14},{1,5},{3,7},{5,9},{7,11},{... | collective-permute-start | bytes 3145736 | tf_op jit(solution)/shard_map/ppermute | solution.py:374
  94.8 1.3 collective-permute-start.21
  96.3 6.0 %collective-permute-start.24 = (bf16[256,2048]{1,0:T(8,128)(2,1)}, bf16[256,2048]{1,0:T(8,128)(2,1)}, u32[]{:S(2)}, u32[]{:S(2)}) collective-permute-start(bf16[256,2048]{1,0:T(8,128)(2,1)} %collective-permute-done.23.rest_2_), channel_id=1, source_target_pairs={{0,4},{2,6},{4,8},{6,10},{8,12},{10,14},{1,5},{3,7},{5,9},{7,11},{... | collective-permute-start | bytes 3145736 | tf_op jit(solution)/shard_map/ppermute | solution.py:374
  102.3 16.4 %collective-permute-done.10.rest_3_ = bf16[256,2048]{1,0:T(8,128)(2,1)} collective-permute-done((bf16[256,2048]{1,0:T(8,128)(2,1)}, bf16[256,2048]{1,0:T(8,128)(2,1)}, u32[]{:S(2)}, u32[]{:S(2)}) %collective-permute-start.10) | collective-permute-done | bytes 1048608 | tf_op jit(solution)/shard_map/ppermute | solution.py:374
  118.7 4.4 %collective-permute-start.11 = (bf16[256,2048]{1,0:T(8,128)(2,1)}, bf16[256,2048]{1,0:T(8,128)(2,1)S(1)}, u32[]{:S(2)}, u32[]{:S(2)}) collective-permute-start(bf16[256,2048]{1,0:T(8,128)(2,1)} %collective-permute-done.10.rest_3_), channel_id=1, source_target_pairs={{0,4},{2,6},{4,8},{6,10},{8,12},{10,14},{1,5},{3,7},{5,9},{7,11},{... | collective-permute-start | bytes 3145736 | tf_op jit(solution)/shard_map/ppermute | solution.py:374
  123.2 1.3 collective-permute-start.8
  124.6 15.6 %collective-permute-done.21.rest_0_ = bf16[256,2048]{1,0:T(8,128)(2,1)S(1)} collective-permute-done((bf16[256,2048]{1,0:T(8,128)(2,1)}, bf16[256,2048]{1,0:T(8,128)(2,1)S(1)}, u32[]{:S(2)}, u32[]{:S(2)}) %collective-permute-start.21) | collective-permute-done | bytes 1048608 | tf_op jit(solution)/shard_map/ppermute | solution.py:374
  140.2 1.3 collective-permute-start.22
  141.5 4.6 %collective-permute-start.25 = (bf16[256,2048]{1,0:T(8,128)(2,1)}, bf16[256,2048]{1,0:T(8,128)(2,1)S(1)}, u32[]{:S(2)}, u32[]{:S(2)}) collective-permute-start(bf16[256,2048]{1,0:T(8,128)(2,1)} %collective-permute-done.24.rest_2_), channel_id=1, source_target_pairs={{0,4},{2,6},{4,8},{6,10},{8,12},{10,14},{1,5},{3,7},{5,9},{7,11},{... | collective-permute-start | bytes 3145736 | tf_op jit(solution)/shard_map/ppermute | solution.py:374
  146.1 17.6 %collective-permute-done.11.rest_3_ = bf16[256,2048]{1,0:T(8,128)(2,1)S(1)} collective-permute-done((bf16[256,2048]{1,0:T(8,128)(2,1)}, bf16[256,2048]{1,0:T(8,128)(2,1)S(1)}, u32[]{:S(2)}, u32[]{:S(2)}) %collective-permute-start.11) | collective-permute-done | bytes 1048608 | tf_op jit(solution)/shard_map/ppermute | solution.py:374
  163.7 5.2 %collective-permute-start.12 = (bf16[256,2048]{1,0:T(8,128)(2,1)S(1)}, bf16[256,2048]{1,0:T(8,128)(2,1)}, u32[]{:S(2)}, u32[]{:S(2)}) collective-permute-start(bf16[256,2048]{1,0:T(8,128)(2,1)S(1)} %collective-permute-done.11.rest_3_), channel_id=1, source_target_pairs={{0,4},{2,6},{4,8},{6,10},{8,12},{10,14},{1,5},{3,7},{5,9},{7,11},{... | collective-permute-start | bytes 3145736 | tf_op jit(solution)/shard_map/ppermute | solution.py:374
  168.9 1.3 collective-permute-start.9
  170.2 17.0 %shard_map.67 = (bf16[256,2048]{1,0:T(8,128)(2,1)S(1)}, bf16[256,2048]{1,0:T(8,128)(2,1)}) custom-call(s32[2]{0:T(128)S(1)} %pad_add_fusion.1.meta, bf16[256,2048]{1,0:T(8,128)(2,1)} %collective-permute-done.20.rest_0_, bf16[256,2048]{1,0:T(8,128)(2,1)} %collective-permute-done.7.rest_1_, bf16[256,2048]{1,0:T(8,128)(2,1)} %collective-permute-done.23.rest_2_, ...), custom_call_target="tpu_custom_call" | custom-call | flops 8589934592 | bytes 16777216 | tf_op jit(solution)/shard_map/pallas_call | solution.py:241
  188.2 1.5 collective-permute-start.31
  189.7 3.4 %copy-done.1 = bf16[4096,1024]{1,0:T(8,128)(2,1)S(1)} copy-done((bf16[4096,1024]{1,0:T(8,128)(2,1)S(1)}, bf16[4096,1024]{1,0:T(8,128)(2,1)}, u32[]{:S(2)}) %copy-start.1) | copy-done | bytes 8388632
  193.1 10.8 %shard_map.68 = (bf16[128,2048]{1,0:T(8,128)(2,1)S(1)}, bf16[128,2048]{1,0:T(8,128)(2,1)}) custom-call(s32[2]{0:T(128)S(1)} %pad_add_fusion.1.meta, bf16[256,2048]{1,0:T(8,128)(2,1)S(1)} %collective-permute-done.21.rest_0_, bf16[256,2048]{1,0:T(8,128)(2,1)S(1)} %collective-permute-done.8.rest_1_, bf16[256,2048]{1,0:T(8,128)(2,1)} %collective-permute-done.24.rest_2_, ...), custom_call_target="tpu_custom_call" | custom-call | flops 4294967296 | bytes 16777216 | tf_op jit(solution)/shard_map/pallas_call | solution.py:241
  205.4 3.4 %copy-done.2 = bf16[4096,1024]{1,0:T(8,128)(2,1)S(1)} copy-done((bf16[4096,1024]{1,0:T(8,128)(2,1)S(1)}, bf16[4096,1024]{1,0:T(8,128)(2,1)}, u32[]{:S(2)}) %copy-start.2) | copy-done | bytes 8388632
  208.8 9.8 %shard_map.69 = bf16[256,2048]{1,0:T(8,128)(2,1)S(1)} custom-call(s32[2]{0:T(128)S(1)} %broadcast_1_meta.2.meta, bf16[256,2048]{1,0:T(8,128)(2,1)S(1)} %copy-done.4, bf16[256,2048]{1,0:T(8,128)(2,1)S(1)} %copy-done.5, bf16[4096,1024]{1,0:T(8,128)(2,1)S(1)} %copy-done.2, bf16[4096,1024]{1,0:T(8,128)(2,1)} %collective-permute-done.26.rest_3_.rest_5_), custom_call_target="tpu_custom_call" | custom-call | flops 4294967296 | bytes 16777216 | tf_op jit(solution)/shard_map/pallas_call | solution.py:241
  219.6 1.5 collective-permute-start.39
  221.1 3.4 %copy-done.3 = bf16[4096,1024]{1,0:T(8,128)(2,1)S(1)} copy-done((bf16[4096,1024]{1,0:T(8,128)(2,1)S(1)}, bf16[4096,1024]{1,0:T(8,128)(2,1)}, u32[]{:S(2)}) %copy-start.3) | copy-done | bytes 8388632
  226.9 6.3 %shard_map.64.rest_2_ = f32[256,2048]{1,0:T(8,128)S(1)} custom-call(s32[2]{0:T(128)S(1)} %pad_add_fusion.1.meta, bf16[256,2048]{1,0:T(8,128)(2,1)S(1)} %copy-done.9, bf16[256,2048]{1,0:T(8,128)(2,1)S(1)} %copy-done.11, bf16[4096,1024]{1,0:T(8,128)(2,1)S(1)} %copy-done.3, bf16[4096,1024]{1,0:T(8,128)(2,1)} %collective-permute-done.26.rest_3_.rest_5_), custom_call_target="tpu_custom_call" | custom-call | flops 2147483648 | bytes 8388608 | tf_op jit(solution)/shard_map/pallas_call | solution.py:241
  233.2 3.7 %shard_map.65 = (bf16[128,1024]{1,0:T(8,128)(2,1)S(1)}, bf16[128,1024]{1,0:T(8,128)(2,1)S(1)}) custom-call(s32[2]{0:T(128)S(1)} %pad_add_fusion.1.meta, bf16[256,2048]{1,0:T(8,128)(2,1)} %collective-permute-done.9.rest_0_, bf16[256,2048]{1,0:T(8,128)(2,1)} %collective-permute-done.12.rest_1_, f32[256,2048]{1,0:T(8,128)S(1)} %shard_map.64.rest_2_, ...), custom_call_target="tpu_custom_call" | custom-call | flops 1073741824 | bytes 4194304 | tf_op jit(solution)/shard_map/pallas_call | solution.py:241
  236.9 3.5 %collective-permute-start.27 = (bf16[128,1024]{1,0:T(8,128)(2,1)S(1)}, bf16[128,1024]{1,0:T(8,128)(2,1)S(1)}, u32[]{:S(2)}, u32[]{:S(2)}) collective-permute-start(bf16[128,1024]{1,0:T(8,128)(2,1)S(1)} %get-tuple-element.14), channel_id=1, source_target_pairs={{0,1},{1,0},{2,3},{3,2},{4,5},{5,4},{6,7},{7,6},{8,9},{9,8},{10,11... | collective-permute-start | bytes 786440 | tf_op jit(solution)/shard_map/ppermute | solution.py:382
  241.6 6.0 %collective-permute-start.37 = (bf16[128,2048]{1,0:T(8,128)(2,1)S(1)}, bf16[128,2048]{1,0:T(8,128)(2,1)S(1)}, u32[]{:S(2)}, u32[]{:S(2)}) collective-permute-start(bf16[128,2048]{1,0:T(8,128)(2,1)S(1)} %add.31), channel_id=1, source_target_pairs={{0,8},{2,10},{4,12},{6,14},{9,1},{11,3},{13,5},{15,7},{16,24},{18,... | collective-permute-start | bytes 1572872 | tf_op jit(solution)/shard_map/ppermute | solution.py:401
  248.3 1.7 add.30
  251.1 2.9 collective-permute-start.32
  254.0 5.1 %shard_map.66 = (bf16[128,1024]{1,0:T(8,128)(2,1)S(1)}, bf16[128,1024]{1,0:T(8,128)(2,1)S(1)}) custom-call(s32[2]{0:T(128)S(1)} %pad_add_fusion.1.meta, bf16[256,2048]{1,0:T(8,128)(2,1)} %collective-permute-done.9.rest_0_, bf16[256,2048]{1,0:T(8,128)(2,1)} %collective-permute-done.12.rest_1_, f32[256,2048]{1,0:T(8,128)S(1)} %shard_map.64.rest_2_, ...), custom_call_target="tpu_custom_call" | custom-call | flops 1073741824 | bytes 4194304 | tf_op jit(solution)/shard_map/pallas_call | solution.py:241
  259.3 16.3 %collective-permute-done.28 = bf16[128,1024]{1,0:T(8,128)(2,1)S(1)} collective-permute-done((bf16[128,1024]{1,0:T(8,128)(2,1)S(1)}, bf16[128,1024]{1,0:T(8,128)(2,1)S(1)}, u32[]{:S(2)}, u32[]{:S(2)}) %collective-permute-start.28) | collective-permute-done | bytes 262176 | tf_op jit(solution)/shard_map/ppermute | solution.py:382
  277.3 1.3 collective-permute-start.34
  278.6 1.3 collective-permute-start.35
  279.9 5.7 %collective-permute-start.29 = (bf16[128,2048]{1,0:T(8,128)(2,1)}, bf16[128,2048]{1,0:T(8,128)(2,1)}, u32[]{:S(2)}, u32[]{:S(2)}) collective-permute-start(bf16[128,2048]{1,0:T(8,128)(2,1)} %pad_maximum_fusion), channel_id=1, source_target_pairs={{0,12},{2,14},{13,1},{15,3},{16,28},{18,30},{29,17},{31,19}} | collective-permute-start | bytes 1572872 | tf_op jit(solution)/shard_map/ppermute | solution.py:401
  285.6 1.5 collective-permute-start.30
  287.7 2.6 add.32.refs_6_
  290.3 15.1 %collective-permute-done.34.refs_2_ = bf16[128,2048]{1,0:T(8,128)(2,1)} collective-permute-done((bf16[128,2048]{1,0:T(8,128)(2,1)}, bf16[128,2048]{1,0:T(8,128)(2,1)}, u32[]{:S(2)}, u32[]{:S(2)}) %collective-permute-start.34) | collective-permute-done | bytes 524320 | tf_op jit(solution)/shard_map/ppermute | solution.py:401
  305.4 2.2 collective-permute-done.35.refs_3_
  307.6 3.6 %collect.1.refs_2_ = bf16[256,4096]{1,0:T(8,128)(2,1)} custom-call(s32[3]{0:T(128)} %pad_add_fusion.meta, bf16[128,2048]{1,0:T(8,128)(2,1)} %copy-done.15, bf16[128,2048]{1,0:T(8,128)(2,1)} %copy-done.16, bf16[128,2048]{1,0:T(8,128)(2,1)} %collective-permute-done.34.refs_2_, bf16[128,2048]{1,0:T(8,128)(2,1)} %collective-permute-done.35.refs_3_, ...), custom_call_target="tpu_custom_call" | custom-call | tf_op jit(solution)/shard_map/collect/pallas_call | solution.py:336
  (137 shorter events, 21.6 us)
Async XLA Ops:
  0.0 45.5 %copy-start = (s32[16,16]{1,0:T(8,128)S(1)}, s32[16,16]{1,0:T(8,128)}, u32[]{:S(2)}) copy-start(s32[16,16]{1,0:T(8,128)} %param.10) | copy-start | bytes 3076
  0.0 31.6 %copy-start.12 = (bf16[256,4096]{1,0:T(8,128)(2,1)S(1)}, bf16[256,4096]{1,0:T(8,128)(2,1)}, u32[]{:S(2)}) copy-start(bf16[256,4096]{1,0:T(8,128)(2,1)} %param.6) | copy-start | bytes 6291460
  0.0 170.2 %collective-permute-start.26 = (bf16[4096,1024]{1,0:T(8,128)(2,1)}, bf16[4096,1024]{1,0:T(8,128)(2,1)}, u32[]{:S(2)}, u32[]{:S(2)}) collective-permute-start(bf16[4096,1024]{1,0:T(8,128)(2,1)} %rest_2_.3), channel_id=1, source_target_pairs={{0,2},{2,0},{4,6},{6,4},{8,10},{10,8},{12,14},{14,12},{1,3},{3,1},... | collective-permute-start | bytes 25165832 | tf_op jit(solution)/shard_map/ppermute | solution.py:378
  1.8 31.3 %copy-start.18 = (bf16[256,512]{1,0:T(8,128)(2,1)}, bf16[256,512]{1,0:T(8,128)(2,1)S(1)}, u32[]{:S(2)}) copy-start(bf16[256,512]{1,0:T(8,128)(2,1)S(1)} %pad_maximum_fusion.2.rest_0_) | copy-start | bytes 786436
  1.8 11.2 %collective-permute-start.13 = (bf16[256,512]{1,0:T(8,128)(2,1)S(1)}, bf16[256,512]{1,0:T(8,128)(2,1)S(1)}, u32[]{:S(2)}, u32[]{:S(2)}) collective-permute-start(bf16[256,512]{1,0:T(8,128)(2,1)S(1)} %pad_maximum_fusion.2.rest_0_), channel_id=1, source_target_pairs={{0,4},{2,6},{4,8},{6,10},{8,12},{10,14},{1,5},{3,7},{5,9},{7,11},{... | collective-permute-start | bytes 786440 | tf_op jit(solution)/shard_map/ppermute | solution.py:374
  6.3 21.0 %collective-permute-start.14 = (bf16[256,512]{1,0:T(8,128)(2,1)S(1)}, bf16[256,512]{1,0:T(8,128)(2,1)S(1)}, u32[]{:S(2)}, u32[]{:S(2)}) collective-permute-start(bf16[256,512]{1,0:T(8,128)(2,1)S(1)} %pad_maximum_fusion.2.rest_0_), channel_id=1, source_target_pairs={{0,8},{2,10},{4,12},{6,14},{1,9},{3,11},{5,13},{7,15},{16,24},{18,... | collective-permute-start | bytes 786440 | tf_op jit(solution)/shard_map/ppermute | solution.py:374
  10.8 22.3 %collective-permute-start.15 = (bf16[256,512]{1,0:T(8,128)(2,1)S(1)}, bf16[256,512]{1,0:T(8,128)(2,1)S(1)}, u32[]{:S(2)}, u32[]{:S(2)}) collective-permute-start(bf16[256,512]{1,0:T(8,128)(2,1)S(1)} %pad_maximum_fusion.2.rest_0_), channel_id=1, source_target_pairs={{0,12},{2,14},{1,13},{3,15},{16,28},{18,30},{17,29},{19,31}} | collective-permute-start | bytes 786440 | tf_op jit(solution)/shard_map/ppermute | solution.py:374
  12.1 32.5 %collective-permute-start.16 = (bf16[256,512]{1,0:T(8,128)(2,1)S(1)}, bf16[256,512]{1,0:T(8,128)(2,1)S(1)}, u32[]{:S(2)}, u32[]{:S(2)}) collective-permute-start(bf16[256,512]{1,0:T(8,128)(2,1)S(1)} %pad_maximum_fusion.2.rest_0_), channel_id=1, source_target_pairs={{0,2},{2,0},{4,6},{6,4},{8,10},{10,8},{12,14},{14,12},{1,3},{3,1},... | collective-permute-start | bytes 786440 | tf_op jit(solution)/shard_map/ppermute | solution.py:378
  12.2 36.3 %copy-start.17 = (bf16[256,512]{1,0:T(8,128)(2,1)}, bf16[256,512]{1,0:T(8,128)(2,1)S(1)}, u32[]{:S(2)}) copy-start(bf16[256,512]{1,0:T(8,128)(2,1)S(1)} %pad_maximum_fusion.1.rest_0_) | copy-start | bytes 786436
  13.0 31.7 %copy-start.22 = (bf16[256,512]{1,0:T(8,128)(2,1)}, bf16[256,512]{1,0:T(8,128)(2,1)S(1)}, u32[]{:S(2)}) copy-start(bf16[256,512]{1,0:T(8,128)(2,1)S(1)} %collective-permute-done.13.rest_1_) | copy-start | bytes 786436
  13.0 31.8 %collective-permute-start = (bf16[256,512]{1,0:T(8,128)(2,1)S(1)}, bf16[256,512]{1,0:T(8,128)(2,1)S(1)}, u32[]{:S(2)}, u32[]{:S(2)}) collective-permute-start(bf16[256,512]{1,0:T(8,128)(2,1)S(1)} %pad_maximum_fusion.1.rest_0_), channel_id=1, source_target_pairs={{0,4},{2,6},{4,8},{6,10},{8,12},{10,14},{1,5},{3,7},{5,9},{7,11},{... | collective-permute-start | bytes 786440 | tf_op jit(solution)/shard_map/ppermute | solution.py:374
  27.3 18.0 %collective-permute-start.1 = (bf16[256,512]{1,0:T(8,128)(2,1)S(1)}, bf16[256,512]{1,0:T(8,128)(2,1)S(1)}, u32[]{:S(2)}, u32[]{:S(2)}) collective-permute-start(bf16[256,512]{1,0:T(8,128)(2,1)S(1)} %pad_maximum_fusion.1.rest_0_), channel_id=1, source_target_pairs={{0,8},{2,10},{4,12},{6,14},{1,9},{3,11},{5,13},{7,15},{16,24},{18,... | collective-permute-start | bytes 786440 | tf_op jit(solution)/shard_map/ppermute | solution.py:374
  33.1 15.4 %collective-permute-start.2 = (bf16[256,512]{1,0:T(8,128)(2,1)S(1)}, bf16[256,512]{1,0:T(8,128)(2,1)S(1)}, u32[]{:S(2)}, u32[]{:S(2)}) collective-permute-start(bf16[256,512]{1,0:T(8,128)(2,1)S(1)} %pad_maximum_fusion.1.rest_0_), channel_id=1, source_target_pairs={{0,12},{2,14},{1,13},{3,15},{16,28},{18,30},{17,29},{19,31}} | collective-permute-start | bytes 786440 | tf_op jit(solution)/shard_map/ppermute | solution.py:374
  44.7 3.9 %collective-permute-start.17 = (bf16[256,512]{1,0:T(8,128)(2,1)S(1)}, bf16[256,512]{1,0:T(8,128)(2,1)S(1)}, u32[]{:S(2)}, u32[]{:S(2)}) collective-permute-start(bf16[256,512]{1,0:T(8,128)(2,1)S(1)} %collective-permute-done.13.rest_1_), channel_id=1, source_target_pairs={{0,2},{2,0},{4,6},{6,4},{8,10},{10,8},{12,14},{14,12},{1,3},{3,1},... | collective-permute-start | bytes 786440 | tf_op jit(solution)/shard_map/ppermute | solution.py:378
  44.8 4.3 %collective-permute-start.18 = (bf16[256,512]{1,0:T(8,128)(2,1)S(1)}, bf16[256,512]{1,0:T(8,128)(2,1)S(1)}, u32[]{:S(2)}, u32[]{:S(2)}) collective-permute-start(bf16[256,512]{1,0:T(8,128)(2,1)S(1)} %collective-permute-done.14.rest_2_), channel_id=1, source_target_pairs={{0,2},{2,0},{4,6},{6,4},{8,10},{10,8},{12,14},{14,12},{1,3},{3,1},... | collective-permute-start | bytes 786440 | tf_op jit(solution)/shard_map/ppermute | solution.py:378
  45.4 3.8 %collective-permute-start.19 = (bf16[256,512]{1,0:T(8,128)(2,1)S(1)}, bf16[256,512]{1,0:T(8,128)(2,1)S(1)}, u32[]{:S(2)}, u32[]{:S(2)}) collective-permute-start(bf16[256,512]{1,0:T(8,128)(2,1)S(1)} %collective-permute-done.15.rest_3_), channel_id=1, source_target_pairs={{0,2},{2,0},{4,6},{6,4},{8,10},{10,8},{12,14},{14,12},{1,3},{3,1},... | collective-permute-start | bytes 786440 | tf_op jit(solution)/shard_map/ppermute | solution.py:378
  48.6 10.4 %collective-permute-start.3 = (bf16[256,512]{1,0:T(8,128)(2,1)S(1)}, bf16[256,512]{1,0:T(8,128)(2,1)S(1)}, u32[]{:S(2)}, u32[]{:S(2)}) collective-permute-start(bf16[256,512]{1,0:T(8,128)(2,1)S(1)} %pad_maximum_fusion.1.rest_0_), channel_id=1, source_target_pairs={{0,2},{2,0},{4,6},{6,4},{8,10},{10,8},{12,14},{14,12},{1,3},{3,1},... | collective-permute-start | bytes 786440 | tf_op jit(solution)/shard_map/ppermute | solution.py:378
  48.6 11.7 %collective-permute-start.4 = (bf16[256,512]{1,0:T(8,128)(2,1)S(1)}, bf16[256,512]{1,0:T(8,128)(2,1)S(1)}, u32[]{:S(2)}, u32[]{:S(2)}) collective-permute-start(bf16[256,512]{1,0:T(8,128)(2,1)S(1)} %collective-permute-done.rest_1_), channel_id=1, source_target_pairs={{0,2},{2,0},{4,6},{6,4},{8,10},{10,8},{12,14},{14,12},{1,3},{3,1},... | collective-permute-start | bytes 786440 | tf_op jit(solution)/shard_map/ppermute | solution.py:378
  49.1 26.5 %collective-permute-start.5 = (bf16[256,512]{1,0:T(8,128)(2,1)S(1)}, bf16[256,512]{1,0:T(8,128)(2,1)S(1)}, u32[]{:S(2)}, u32[]{:S(2)}) collective-permute-start(bf16[256,512]{1,0:T(8,128)(2,1)S(1)} %collective-permute-done.1.rest_2_), channel_id=1, source_target_pairs={{0,2},{2,0},{4,6},{6,4},{8,10},{10,8},{12,14},{14,12},{1,3},{3,1},... | collective-permute-start | bytes 786440 | tf_op jit(solution)/shard_map/ppermute | solution.py:378
  49.2 26.4 %collective-permute-start.6 = (bf16[256,512]{1,0:T(8,128)(2,1)S(1)}, bf16[256,512]{1,0:T(8,128)(2,1)S(1)}, u32[]{:S(2)}, u32[]{:S(2)}) collective-permute-start(bf16[256,512]{1,0:T(8,128)(2,1)S(1)} %collective-permute-done.2.rest_3_), channel_id=1, source_target_pairs={{0,2},{2,0},{4,6},{6,4},{8,10},{10,8},{12,14},{14,12},{1,3},{3,1},... | collective-permute-start | bytes 786440 | tf_op jit(solution)/shard_map/ppermute | solution.py:378
  59.0 35.8 %collective-permute-start.20 = (bf16[256,2048]{1,0:T(8,128)(2,1)}, bf16[256,2048]{1,0:T(8,128)(2,1)}, u32[]{:S(2)}, u32[]{:S(2)}) collective-permute-start(bf16[256,2048]{1,0:T(8,128)(2,1)} %attend.3.rest_0_), channel_id=1, source_target_pairs={{4,0},{6,2},{8,4},{10,6},{12,8},{14,10},{5,1},{7,3},{9,5},{11,7},{... | collective-permute-start | bytes 3145736 | tf_op jit(solution)/shard_map/ppermute | solution.py:374
  60.4 35.9 %collective-permute-start.23 = (bf16[256,2048]{1,0:T(8,128)(2,1)}, bf16[256,2048]{1,0:T(8,128)(2,1)}, u32[]{:S(2)}, u32[]{:S(2)}) collective-permute-start(bf16[256,2048]{1,0:T(8,128)(2,1)} %attend.3.rest_0_), channel_id=1, source_target_pairs={{0,4},{2,6},{4,8},{6,10},{8,12},{10,14},{1,5},{3,7},{5,9},{7,11},{... | collective-permute-start | bytes 3145736 | tf_op jit(solution)/shard_map/ppermute | solution.py:374
  84.4 34.4 %collective-permute-start.10 = (bf16[256,2048]{1,0:T(8,128)(2,1)}, bf16[256,2048]{1,0:T(8,128)(2,1)}, u32[]{:S(2)}, u32[]{:S(2)}) collective-permute-start(bf16[256,2048]{1,0:T(8,128)(2,1)} %attend.2.rest_1_), channel_id=1, source_target_pairs={{0,4},{2,6},{4,8},{6,10},{8,12},{10,14},{1,5},{3,7},{5,9},{7,11},{... | collective-permute-start | bytes 3145736 | tf_op jit(solution)/shard_map/ppermute | solution.py:374
  93.5 29.7 %collective-permute-start.7 = (bf16[256,2048]{1,0:T(8,128)(2,1)}, bf16[256,2048]{1,0:T(8,128)(2,1)}, u32[]{:S(2)}, u32[]{:S(2)}) collective-permute-start(bf16[256,2048]{1,0:T(8,128)(2,1)} %attend.2.rest_1_), channel_id=1, source_target_pairs={{4,0},{6,2},{8,4},{10,6},{12,8},{14,10},{5,1},{7,3},{9,5},{11,7},{... | collective-permute-start | bytes 3145736 | tf_op jit(solution)/shard_map/ppermute | solution.py:374
  94.8 45.4 %collective-permute-start.21 = (bf16[256,2048]{1,0:T(8,128)(2,1)}, bf16[256,2048]{1,0:T(8,128)(2,1)S(1)}, u32[]{:S(2)}, u32[]{:S(2)}) collective-permute-start(bf16[256,2048]{1,0:T(8,128)(2,1)} %collective-permute-done.20.rest_0_), channel_id=1, source_target_pairs={{4,0},{6,2},{8,4},{10,6},{12,8},{14,10},{5,1},{7,3},{9,5},{11,7},{... | collective-permute-start | bytes 3145736 | tf_op jit(solution)/shard_map/ppermute | solution.py:374
  96.3 45.2 %collective-permute-start.24 = (bf16[256,2048]{1,0:T(8,128)(2,1)}, bf16[256,2048]{1,0:T(8,128)(2,1)}, u32[]{:S(2)}, u32[]{:S(2)}) collective-permute-start(bf16[256,2048]{1,0:T(8,128)(2,1)} %collective-permute-done.23.rest_2_), channel_id=1, source_target_pairs={{0,4},{2,6},{4,8},{6,10},{8,12},{10,14},{1,5},{3,7},{5,9},{7,11},{... | collective-permute-start | bytes 3145736 | tf_op jit(solution)/shard_map/ppermute | solution.py:374
  118.7 44.9 %collective-permute-start.11 = (bf16[256,2048]{1,0:T(8,128)(2,1)}, bf16[256,2048]{1,0:T(8,128)(2,1)S(1)}, u32[]{:S(2)}, u32[]{:S(2)}) collective-permute-start(bf16[256,2048]{1,0:T(8,128)(2,1)} %collective-permute-done.10.rest_3_), channel_id=1, source_target_pairs={{0,4},{2,6},{4,8},{6,10},{8,12},{10,14},{1,5},{3,7},{5,9},{7,11},{... | collective-permute-start | bytes 3145736 | tf_op jit(solution)/shard_map/ppermute | solution.py:374
  123.2 45.7 %collective-permute-start.8 = (bf16[256,2048]{1,0:T(8,128)(2,1)}, bf16[256,2048]{1,0:T(8,128)(2,1)S(1)}, u32[]{:S(2)}, u32[]{:S(2)}) collective-permute-start(bf16[256,2048]{1,0:T(8,128)(2,1)} %collective-permute-done.7.rest_1_), channel_id=1, source_target_pairs={{4,0},{6,2},{8,4},{10,6},{12,8},{14,10},{5,1},{7,3},{9,5},{11,7},{... | collective-permute-start | bytes 3145736 | tf_op jit(solution)/shard_map/ppermute | solution.py:374
  140.2 63.7 %collective-permute-start.22 = (bf16[256,2048]{1,0:T(8,128)(2,1)S(1)}, bf16[256,2048]{1,0:T(8,128)(2,1)S(1)}, u32[]{:S(2)}, u32[]{:S(2)}) collective-permute-start(bf16[256,2048]{1,0:T(8,128)(2,1)S(1)} %collective-permute-done.21.rest_0_), channel_id=1, source_target_pairs={{4,0},{6,2},{8,4},{10,6},{12,8},{14,10},{5,1},{7,3},{9,5},{11,7},{... | collective-permute-start | bytes 3145736 | tf_op jit(solution)/shard_map/ppermute | solution.py:374
  141.5 77.1 %collective-permute-start.25 = (bf16[256,2048]{1,0:T(8,128)(2,1)}, bf16[256,2048]{1,0:T(8,128)(2,1)S(1)}, u32[]{:S(2)}, u32[]{:S(2)}) collective-permute-start(bf16[256,2048]{1,0:T(8,128)(2,1)} %collective-permute-done.24.rest_2_), channel_id=1, source_target_pairs={{0,4},{2,6},{4,8},{6,10},{8,12},{10,14},{1,5},{3,7},{5,9},{7,11},{... | collective-permute-start | bytes 3145736 | tf_op jit(solution)/shard_map/ppermute | solution.py:374
  163.7 69.5 %collective-permute-start.12 = (bf16[256,2048]{1,0:T(8,128)(2,1)S(1)}, bf16[256,2048]{1,0:T(8,128)(2,1)}, u32[]{:S(2)}, u32[]{:S(2)}) collective-permute-start(bf16[256,2048]{1,0:T(8,128)(2,1)S(1)} %collective-permute-done.11.rest_3_), channel_id=1, source_target_pairs={{0,4},{2,6},{4,8},{6,10},{8,12},{10,14},{1,5},{3,7},{5,9},{7,11},{... | collective-permute-start | bytes 3145736 | tf_op jit(solution)/shard_map/ppermute | solution.py:374
  168.9 64.3 %collective-permute-start.9 = (bf16[256,2048]{1,0:T(8,128)(2,1)S(1)}, bf16[256,2048]{1,0:T(8,128)(2,1)}, u32[]{:S(2)}, u32[]{:S(2)}) collective-permute-start(bf16[256,2048]{1,0:T(8,128)(2,1)S(1)} %collective-permute-done.8.rest_1_), channel_id=1, source_target_pairs={{4,0},{6,2},{8,4},{10,6},{12,8},{14,10},{5,1},{7,3},{9,5},{11,7},{... | collective-permute-start | bytes 3145736 | tf_op jit(solution)/shard_map/ppermute | solution.py:374
  188.2 60.1 %collective-permute-start.31 = (bf16[256,2048]{1,0:T(8,128)(2,1)}, bf16[256,2048]{1,0:T(8,128)(2,1)}, u32[]{:S(2)}, u32[]{:S(2)}) collective-permute-start(bf16[256,2048]{1,0:T(8,128)(2,1)} %get-tuple-element.18), channel_id=1, source_target_pairs={{0,1},{1,0},{2,3},{3,2},{4,5},{5,4},{6,7},{7,6},{8,9},{9,8},{10,11... | collective-permute-start | bytes 3145736 | tf_op jit(solution)/shard_map/ppermute | solution.py:382
  193.1 40.1 %slice-start = ((s8[8388608]{0:T(1024)(128)(4,1)}), s8[4194304]{0:T(1024)(128)(4,1)S(1)}, s32[]{:S(2)}) async-start(s8[8388608]{0:T(1024)(128)(4,1)} %bitcast.8), calls=%async_computation | async-start | bytes 8388608
  204.9 35.5 %collective-permute-start.36 = (bf16[128,2048]{1,0:T(8,128)(2,1)}, bf16[128,2048]{1,0:T(8,128)(2,1)}, u32[]{:S(2)}, u32[]{:S(2)}) collective-permute-start(bf16[128,2048]{1,0:T(8,128)(2,1)} %get-tuple-element.20), channel_id=1, source_target_pairs={{0,1},{1,0},{2,3},{3,2},{4,5},{5,4},{6,7},{7,6},{8,9},{9,8},{10,11... | collective-permute-start | bytes 1572872 | tf_op jit(solution)/shard_map/ppermute | solution.py:382
  219.6 57.7 %collective-permute-start.39 = (bf16[256,2048]{1,0:T(8,128)(2,1)S(1)}, bf16[256,2048]{1,0:T(8,128)(2,1)}, u32[]{:S(2)}, u32[]{:S(2)}) collective-permute-start(bf16[256,2048]{1,0:T(8,128)(2,1)S(1)} %shard_map.69), channel_id=1, source_target_pairs={{1,0},{3,2},{5,4},{7,6},{8,9},{10,11},{12,13},{14,15},{17,16},{19,... | collective-permute-start | bytes 3145736 | tf_op jit(solution)/shard_map/ppermute | solution.py:442
  236.9 22.2 %collective-permute-start.27 = (bf16[128,1024]{1,0:T(8,128)(2,1)S(1)}, bf16[128,1024]{1,0:T(8,128)(2,1)S(1)}, u32[]{:S(2)}, u32[]{:S(2)}) collective-permute-start(bf16[128,1024]{1,0:T(8,128)(2,1)S(1)} %get-tuple-element.14), channel_id=1, source_target_pairs={{0,1},{1,0},{2,3},{3,2},{4,5},{5,4},{6,7},{7,6},{8,9},{9,8},{10,11... | collective-permute-start | bytes 786440 | tf_op jit(solution)/shard_map/ppermute | solution.py:382
  241.6 37.0 %collective-permute-start.37 = (bf16[128,2048]{1,0:T(8,128)(2,1)S(1)}, bf16[128,2048]{1,0:T(8,128)(2,1)S(1)}, u32[]{:S(2)}, u32[]{:S(2)}) collective-permute-start(bf16[128,2048]{1,0:T(8,128)(2,1)S(1)} %add.31), channel_id=1, source_target_pairs={{0,8},{2,10},{4,12},{6,14},{9,1},{11,3},{13,5},{15,7},{16,24},{18,... | collective-permute-start | bytes 1572872 | tf_op jit(solution)/shard_map/ppermute | solution.py:401
  247.6 32.3 %collective-permute-start.38 = (bf16[128,2048]{1,0:T(8,128)(2,1)S(1)}, bf16[128,2048]{1,0:T(8,128)(2,1)S(1)}, u32[]{:S(2)}, u32[]{:S(2)}) collective-permute-start(bf16[128,2048]{1,0:T(8,128)(2,1)S(1)} %add.31), channel_id=1, source_target_pairs={{1,8},{3,10},{5,12},{7,14},{8,1},{10,3},{12,5},{14,7},{17,24},{19,... | collective-permute-start | bytes 1572872 | tf_op jit(solution)/shard_map/ppermute | solution.py:402
  251.1 34.5 %collective-permute-start.32 = (bf16[128,2048]{1,0:T(8,128)(2,1)}, bf16[128,2048]{1,0:T(8,128)(2,1)S(1)}, u32[]{:S(2)}, u32[]{:S(2)}) collective-permute-start(bf16[128,2048]{1,0:T(8,128)(2,1)} %get-tuple-element.24), channel_id=1, source_target_pairs={{0,4},{2,6},{4,8},{6,10},{9,5},{11,7},{13,9},{15,11},{16,20},{18,2... | collective-permute-start | bytes 1572872 | tf_op jit(solution)/shard_map/ppermute | solution.py:401
  259.2 16.5 %collective-permute-start.28 = (bf16[128,1024]{1,0:T(8,128)(2,1)S(1)}, bf16[128,1024]{1,0:T(8,128)(2,1)S(1)}, u32[]{:S(2)}, u32[]{:S(2)}) collective-permute-start(bf16[128,1024]{1,0:T(8,128)(2,1)S(1)} %get-tuple-element.16), channel_id=1, source_target_pairs={{0,1},{1,0},{2,3},{3,2},{4,5},{5,4},{6,7},{7,6},{8,9},{9,8},{10,11... | collective-permute-start | bytes 786440 | tf_op jit(solution)/shard_map/ppermute | solution.py:382
  276.6 13.7 %collective-permute-start.33 = (bf16[128,2048]{1,0:T(8,128)(2,1)}, bf16[128,2048]{1,0:T(8,128)(2,1)S(1)}, u32[]{:S(2)}, u32[]{:S(2)}) collective-permute-start(bf16[128,2048]{1,0:T(8,128)(2,1)} %get-tuple-element.24), channel_id=1, source_target_pairs={{1,4},{3,6},{5,8},{7,10},{8,5},{10,7},{12,9},{14,11},{17,20},{19,2... | collective-permute-start | bytes 1572872 | tf_op jit(solution)/shard_map/ppermute | solution.py:402
  277.3 28.1 %collective-permute-start.34 = (bf16[128,2048]{1,0:T(8,128)(2,1)}, bf16[128,2048]{1,0:T(8,128)(2,1)}, u32[]{:S(2)}, u32[]{:S(2)}) collective-permute-start(bf16[128,2048]{1,0:T(8,128)(2,1)} %get-tuple-element.23), channel_id=1, source_target_pairs={{4,0},{6,2},{9,13},{11,15},{20,16},{22,18},{25,29},{27,31}} | collective-permute-start | bytes 1572872 | tf_op jit(solution)/shard_map/ppermute | solution.py:401
  278.6 29.0 %copy-start.13 = (bf16[128,2048]{1,0:T(8,128)(2,1)}, bf16[128,2048]{1,0:T(8,128)(2,1)S(1)}, u32[]{:S(2)}) copy-start(bf16[128,2048]{1,0:T(8,128)(2,1)S(1)} %collective-permute-done.37.refs_4_) | copy-start | bytes 1572868
  278.6 29.0 %collective-permute-start.35 = (bf16[128,2048]{1,0:T(8,128)(2,1)}, bf16[128,2048]{1,0:T(8,128)(2,1)}, u32[]{:S(2)}, u32[]{:S(2)}) collective-permute-start(bf16[128,2048]{1,0:T(8,128)(2,1)} %get-tuple-element.23), channel_id=1, source_target_pairs={{5,0},{7,2},{8,13},{10,15},{21,16},{23,18},{24,29},{26,31}} | collective-permute-start | bytes 1572872 | tf_op jit(solution)/shard_map/ppermute | solution.py:402
  279.9 27.7 %copy-start.14 = (bf16[128,2048]{1,0:T(8,128)(2,1)}, bf16[128,2048]{1,0:T(8,128)(2,1)S(1)}, u32[]{:S(2)}) copy-start(bf16[128,2048]{1,0:T(8,128)(2,1)S(1)} %collective-permute-done.38.refs_5_) | copy-start | bytes 1572868
  279.9 31.3 %collective-permute-start.29 = (bf16[128,2048]{1,0:T(8,128)(2,1)}, bf16[128,2048]{1,0:T(8,128)(2,1)}, u32[]{:S(2)}, u32[]{:S(2)}) collective-permute-start(bf16[128,2048]{1,0:T(8,128)(2,1)} %pad_maximum_fusion), channel_id=1, source_target_pairs={{0,12},{2,14},{13,1},{15,3},{16,28},{18,30},{29,17},{31,19}} | collective-permute-start | bytes 1572872 | tf_op jit(solution)/shard_map/ppermute | solution.py:401
  285.6 25.6 %collective-permute-start.30 = (bf16[128,2048]{1,0:T(8,128)(2,1)}, bf16[128,2048]{1,0:T(8,128)(2,1)}, u32[]{:S(2)}, u32[]{:S(2)}) collective-permute-start(bf16[128,2048]{1,0:T(8,128)(2,1)} %pad_maximum_fusion), channel_id=1, source_target_pairs={{1,12},{3,14},{12,1},{14,3},{17,28},{19,30},{28,17},{30,19}} | collective-permute-start | bytes 1572872 | tf_op jit(solution)/shard_map/ppermute | solution.py:402
  (28 other events, 255.4 us)
